TPU v7x, 32 devices: a whole 2x2x4 slice. The times are simulated.
32 devices in a mesh: dp: 2 (over x), context: 4 (over z), tensor: 4 (over y, core).
Axes of the slice: x: 2, y: 2, z: 4, core: 2. Of those that a mesh axis runs over, the one named last changes fastest.
Arguments:
- tokens: bfloat16 [6144, 640], P(('dp', 'context')), may hold values from -8 to 8
- seq_lengths: int32 [2, 2], P('dp'), may hold values from 1 to 2048, 3072 in all within a row
- input_gain: bfloat16 [640], P('dp'), may hold values from 0.25 to 1.75
- query_weight: bfloat16 [640, 1024], P('dp', 'tensor'), may hold values from -0.25 to 0.25
- key_weight: bfloat16 [640, 256], P('dp'), may hold values from -0.25 to 0.25
- value_weight: bfloat16 [640, 256], P('dp'), may hold values from -0.25 to 0.25
- query_gain: bfloat16 [256], P('dp'), may hold values from 0.25 to 1.75
- key_gain: bfloat16 [256], P('dp'), may hold values from 0.25 to 1.75
- output_weight: bfloat16 [1024, 640], P('tensor', 'dp'), may hold values from -0.1875 to 0.1875
- attention_gain: bfloat16 [640], P('dp'), may hold values from 0.25 to 1.75
- prefeed_gain: bfloat16 [640], P('dp'), may hold values from 0.25 to 1.75
- gate_weight: bfloat16 [640, 2048], P('dp', 'tensor'), may hold values from -0.25 to 0.25
- up_weight: bfloat16 [640, 2048], P('dp', 'tensor'), may hold values from -0.25 to 0.25
- down_weight: bfloat16 [2048, 640], P('tensor', 'dp'), may hold values from -0.125 to 0.125
- feed_gain: bfloat16 [640], P('dp'), may hold values from 0.25 to 1.75
- cotangent: bfloat16 [6144, 640], P(('dp', 'context')), may hold values from -8 to 8
Outputs:
- layer_out: bfloat16 [6144, 640], P(('dp', 'context'))
- tokens_grad: float32 [6144, 640], P(('dp', 'context'))
- input_gain_grad: float32 [640], P('dp')
- query_weight_grad: float32 [640, 1024], P('dp', 'tensor')
- key_weight_grad: float32 [640, 256], P('dp')
- value_weight_grad: float32 [640, 256], P('dp')
- query_gain_grad: float32 [256], P('dp')
- key_gain_grad: float32 [256], P('dp')
- output_weight_grad: float32 [1024, 640], P('tensor', 'dp')
- attention_gain_grad: float32 [640], P('dp')
- prefeed_gain_grad: float32 [640], P('dp')
- gate_weight_grad: float32 [640, 2048], P('dp', 'tensor')
- up_weight_grad: float32 [640, 2048], P('dp', 'tensor')
- down_weight_grad: float32 [2048, 640], P('tensor', 'dp')
- feed_gain_grad: float32 [640], P('dp')
Inputs may be any that keep to these rules, and one draw needn't show every extreme that they name: `seq_lengths`: each row lists 2 lengths that add up to 3072, none above 2048.
All inputs are finite; a program needn't handle non-finite values.
Results may differ from a plain program's by a relative error of at most 0.022.
Values may be sent and summed in bfloat16 or wider, within the bound.
No kernel may reach another device: no remote copies, remote signals or barrier semaphores. Data moves between devices by JAX's collectives and lax.ppermute only.
A program may use at most 128 MiB of HBM per device.

v0:
```python
import math

import jax
import jax.numpy as jnp
from jax import lax
from jax.sharding import PartitionSpec as P

HD = 256
LMAX = 2048


EPS = 1e-06
NEG = -1000000000.0
SCALE = 0.0625


def passed_along(array, axis, by):
    devices = lax.axis_size(axis)
    pairs = [(i, i + by) for i in range(devices) if 0 <= i + by < devices]
    return lax.ppermute(array, axis, pairs)


def shortened(array):

    def short(part):
        return part.astype(jnp.bfloat16) if part.dtype == jnp.float32 else part

    return jax.tree.map(short, array)


def product(left_side, right_side):
    return jnp.dot(left_side, right_side, preferred_element_type=jnp.float32)


def product_lt(left_side, right_side):
    return lax.dot_general(
        left_side, right_side, (((0,), (0,)), ((), ())), preferred_element_type=jnp.float32
    )


def product_rt(left_side, right_side):
    return lax.dot_general(
        left_side, right_side, (((1,), (1,)), ((), ())), preferred_element_type=jnp.float32
    )


def rms_norm(values, scale_gain):
    return values * lax.rsqrt(jnp.mean(values * values, axis=-1, keepdims=True) + EPS) * scale_gain


def rotate(values, position):
    half_width = values.shape[-1] // 2
    frequency = jnp.exp(
        jnp.arange(half_width, dtype=jnp.float32) * (-2.0 * math.log(1000000.0) / values.shape[-1])
    )
    angles = position.astype(jnp.float32).reshape((-1,) + (1,) * (values.ndim - 1)) * frequency
    cosines = jnp.cos(angles)
    sines = jnp.sin(angles)
    first_half = values[..., :half_width]
    second_half = values[..., half_width:]
    return jnp.concatenate(
        [first_half * cosines - second_half * sines, second_half * cosines + first_half * sines],
        axis=-1,
    )


def layout(lengths, row_index):
    seq_ends = jnp.cumsum(lengths)
    starts = seq_ends - lengths
    member = (
        (row_index[:, None] >= starts[None, :]) & (row_index[:, None] < seq_ends[None, :])
    ).astype(jnp.int32)
    number = jnp.arange(lengths.shape[0], dtype=jnp.int32)
    segment = jnp.sum(member * (number[None, :] + 1), axis=1) - 1
    position = row_index - jnp.sum(member * starts[None, :], axis=1)
    return (segment, position)


def block_scores(query, key_block, allowed):
    scores = jnp.einsum("qhd,kd->hqk", query, key_block, preferred_element_type=jnp.float32) * SCALE
    return jnp.where(allowed[None], scores, NEG)


def local(
    tokens,
    seq_lengths,
    input_gain,
    query_weight,
    key_weight,
    value_weight,
    query_gain,
    key_gain,
    output_weight,
    attention_gain,
    prefeed_gain,
    gate_weight,
    up_weight,
    down_weight,
    feed_gain,
    cotangent,
):
    row_count = tokens.shape[0]
    chain_width = lax.axis_size("context")
    chain_place = lax.axis_index("context")
    chain_reach = min(chain_width - 1, (LMAX - 2) // row_count + 1)
    lengths = seq_lengths[0]
    own_index = chain_place * row_count + jnp.arange(row_count, dtype=jnp.int32)
    own_segment, own_position = layout(lengths, own_index)
    w_query, w_key, w_value, w_output, g_input, g_attention, g_query, g_key = (
        lax.all_gather(query_weight, "dp", axis=0, tiled=True),
        lax.all_gather(key_weight, "dp", axis=0, tiled=True),
        lax.all_gather(value_weight, "dp", axis=0, tiled=True),
        lax.all_gather(output_weight, "dp", axis=1, tiled=True),
        lax.all_gather(input_gain, "dp", axis=0, tiled=True),
        lax.all_gather(attention_gain, "dp", axis=0, tiled=True),
        lax.all_gather(query_gain, "dp", axis=0, tiled=True),
        lax.all_gather(key_gain, "dp", axis=0, tiled=True),
    )
    w_gate, w_up, w_down, g_prefeed, g_feed = (
        lax.all_gather(gate_weight, "dp", axis=0, tiled=True),
        lax.all_gather(up_weight, "dp", axis=0, tiled=True),
        lax.all_gather(down_weight, "dp", axis=1, tiled=True),
        lax.all_gather(prefeed_gain, "dp", axis=0, tiled=True),
        lax.all_gather(feed_gain, "dp", axis=0, tiled=True),
    )
    g_input = g_input.astype(jnp.float32)
    g_attention = g_attention.astype(jnp.float32)
    g_query = g_query.astype(jnp.float32)
    g_key = g_key.astype(jnp.float32)
    g_prefeed = g_prefeed.astype(jnp.float32)
    g_feed = g_feed.astype(jnp.float32)
    local_heads = w_query.shape[1] // HD
    stream = tokens.astype(jnp.float32)
    normed_full, input_back = jax.vjp(rms_norm, stream, g_input)
    normed = normed_full.astype(jnp.bfloat16)
    query_raw = product(normed, w_query).reshape(row_count, local_heads, HD)
    key_raw = product(normed, w_key)
    value = product(normed, w_value).astype(jnp.bfloat16)
    query_full, query_back = jax.vjp(
        lambda raw_part, gain_part: rotate(rms_norm(raw_part, gain_part), own_position),
        query_raw,
        g_query,
    )
    key_full, key_back = jax.vjp(
        lambda raw_part, gain_part: rotate(rms_norm(raw_part, gain_part), own_position),
        key_raw,
        g_key,
    )
    query = query_full.astype(jnp.bfloat16)
    key_rot = key_full.astype(jnp.bfloat16)
    blocks = []
    current = (key_rot, value)
    for step in range(chain_reach + 1):
        if step > 0:
            current = passed_along((current[0], current[1]), "context", 1)
        block_index = own_index - step * row_count
        block_segment = layout(lengths, block_index)[0]
        allowed = (own_segment[:, None] == block_segment[None, :]) & (
            block_index[None, :] <= own_index[:, None]
        )
        is_live = own_segment[0] == block_segment[row_count - 1]
        blocks.append((current[0], current[1], allowed, is_live))
    score_shape = (local_heads, row_count, row_count)
    kept_scores = []
    running_max = None
    total_mass = None
    for step in range(chain_reach + 1):
        key_block, value_block, allowed, is_live = blocks[step]

        def compute_block(key_block=key_block, allowed=allowed):
            scores = block_scores(query, key_block, allowed)
            peak = jnp.max(scores, axis=-1)
            return (scores, peak, jnp.sum(jnp.exp(scores - peak[..., None]), axis=-1))

        if step == 0:
            scores, peak, mass = compute_block()
            running_max, total_mass = (peak, mass)
        else:
            scores, peak, mass = compute_block()
            new_max = jnp.maximum(running_max, peak)
            total_mass = total_mass * jnp.exp(running_max - new_max) + mass * jnp.exp(
                peak - new_max
            )
            running_max = new_max
        kept_scores.append(scores)
    log_mass = running_max + jnp.log(total_mass)
    heads_out = jnp.zeros((row_count, local_heads, HD), jnp.float32)
    for step in range(chain_reach + 1):
        key_block, value_block, allowed, is_live = blocks[step]

        def compute_block(value_block=value_block, scores=kept_scores[step]):
            attn_probs = jnp.exp(scores - log_mass[..., None]).astype(jnp.bfloat16)
            return jnp.einsum(
                "hqk,kd->qhd", attn_probs, value_block, preferred_element_type=jnp.float32
            )

        if step == 0:
            heads_out = compute_block()
        else:
            heads_out = heads_out + compute_block()
    heads_low = heads_out.astype(jnp.bfloat16).reshape(row_count, local_heads * HD)
    attn_sum = lax.psum(product(heads_low, w_output).astype(jnp.bfloat16), "tensor").astype(
        jnp.float32
    )
    attn_post, attn_back = jax.vjp(rms_norm, attn_sum, g_attention)
    middle = stream + attn_post
    normed_feed_full, prefeed_back = jax.vjp(rms_norm, middle, g_prefeed)
    normed_feed = normed_feed_full.astype(jnp.bfloat16)
    gate_proj = product(normed_feed, w_gate)
    up_proj = product(normed_feed, w_up)
    activation, activation_back = jax.vjp(
        lambda gate_part, up_part: jax.nn.gelu(gate_part, approximate=True) * up_part,
        gate_proj,
        up_proj,
    )
    hidden = activation.astype(jnp.bfloat16)
    feed_sum = lax.psum(product(hidden, w_down).astype(jnp.bfloat16), "tensor").astype(jnp.float32)
    feed_post, feed_back = jax.vjp(rms_norm, feed_sum, g_feed)
    result = middle + feed_post
    layer_out = result.astype(jnp.bfloat16)
    grad_out = cotangent.astype(jnp.float32)
    grad_feed_full, grad_gfeed = feed_back(grad_out)
    grad_feed = grad_feed_full.astype(jnp.bfloat16)
    grad_wdown = product_lt(hidden, grad_feed)
    grad_hidden = product_rt(grad_feed, w_down)
    grad_gate_full, grad_up_full = activation_back(grad_hidden)
    grad_gate = grad_gate_full.astype(jnp.bfloat16)
    grad_up = grad_up_full.astype(jnp.bfloat16)
    grad_wgate = product_lt(normed_feed, grad_gate)
    grad_wup = product_lt(normed_feed, grad_up)
    grad_normed_feed = lax.psum(
        (product_rt(grad_gate, w_gate) + product_rt(grad_up, w_up)).astype(jnp.bfloat16), "tensor"
    ).astype(jnp.float32)
    grad_middle_norm, grad_gprefeed = prefeed_back(grad_normed_feed)
    grad_middle = grad_out + grad_middle_norm
    grad_attn_full, grad_gattention = attn_back(grad_middle)
    grad_attn = grad_attn_full.astype(jnp.bfloat16)
    grad_woutput = product_lt(heads_low, grad_attn)
    grad_heads = (
        product_rt(grad_attn, w_output).reshape(row_count, local_heads, HD).astype(jnp.bfloat16)
    )
    kept_blocks = []
    row_dots = jnp.zeros(score_shape[:2], jnp.float32)
    for step in range(chain_reach + 1):
        key_block, value_block, allowed, is_live = blocks[step]

        def compute_block(key_block=key_block, value_block=value_block, allowed=allowed):
            scores = block_scores(query, key_block, allowed)
            attn_probs = jnp.exp(scores - log_mass[..., None])
            prob_grad = jnp.einsum(
                "qhd,kd->hqk", grad_heads, value_block, preferred_element_type=jnp.float32
            )
            return (attn_probs, prob_grad, jnp.sum(attn_probs * prob_grad, axis=-1))

        if step == 0:
            attn_probs, prob_grad, partial_dots = compute_block()
        else:
            attn_probs, prob_grad, partial_dots = compute_block()
        row_dots = row_dots + partial_dots
        kept_blocks.append((attn_probs, prob_grad))
    grad_query = jnp.zeros((row_count, local_heads, HD), jnp.float32)
    carried = (jnp.zeros((row_count, HD), jnp.float32), jnp.zeros((row_count, HD), jnp.float32))
    for step in range(chain_reach, -1, -1):
        key_block, value_block, allowed, is_live = blocks[step]
        attn_probs, prob_grad = kept_blocks[step]

        def compute_block(key_block=key_block, attn_probs=attn_probs, prob_grad=prob_grad):
            grad_scores = (attn_probs * (prob_grad - row_dots[..., None])).astype(jnp.bfloat16)
            probs_low = attn_probs.astype(jnp.bfloat16)
            query_part = (
                jnp.einsum(
                    "hqk,kd->qhd", grad_scores, key_block, preferred_element_type=jnp.float32
                )
                * SCALE
            )
            key_part = (
                jnp.einsum("hqk,qhd->kd", grad_scores, query, preferred_element_type=jnp.float32)
                * SCALE
            )
            value_part = jnp.einsum(
                "hqk,qhd->kd", probs_low, grad_heads, preferred_element_type=jnp.float32
            )
            return (query_part, key_part, value_part)

        if step == 0:
            query_part, key_part, value_part = compute_block()
        else:
            query_part, key_part, value_part = compute_block()
        grad_query = grad_query + query_part
        carried = (carried[0] + key_part, carried[1] + value_part)
        if step > 0:
            carried = passed_along((shortened(carried[0]), shortened(carried[1])), "context", -1)
    grad_key, grad_value = (
        lax.psum(carried[0].astype(jnp.bfloat16), "tensor").astype(jnp.float32),
        lax.psum(carried[1].astype(jnp.bfloat16), "tensor").astype(jnp.float32),
    )
    grad_query_full, grad_gquery_part = query_back(grad_query)
    grad_key_full, grad_gkey = key_back(grad_key)
    grad_query_raw = grad_query_full.reshape(row_count, local_heads * HD).astype(jnp.bfloat16)
    grad_key_raw = grad_key_full.astype(jnp.bfloat16)
    grad_value_low = grad_value.astype(jnp.bfloat16)
    grad_wquery = product_lt(normed, grad_query_raw)
    grad_wkey = product_lt(normed, grad_key_raw)
    grad_wvalue = product_lt(normed, grad_value_low)
    grad_normed_part = product_rt(grad_query_raw, w_query)
    grad_normed_sum, grad_gquery = (
        lax.psum(grad_normed_part.astype(jnp.bfloat16), "tensor").astype(jnp.float32),
        lax.psum(grad_gquery_part.astype(jnp.bfloat16), "tensor").astype(jnp.float32),
    )
    grad_normed = (
        grad_normed_sum + product_rt(grad_key_raw, w_key) + product_rt(grad_value_low, w_value)
    )
    grad_stream_norm, grad_ginput = input_back(grad_normed)
    tokens_grad = grad_middle + grad_stream_norm
    totals = lax.psum(
        (
            grad_ginput,
            grad_wquery,
            grad_wkey,
            grad_wvalue,
            grad_gquery,
            grad_gkey,
            grad_woutput,
            grad_gattention,
            grad_gprefeed,
            grad_wgate,
            grad_wup,
            grad_wdown,
            grad_gfeed,
        ),
        ("dp", "context"),
    )
    shard_place = lax.axis_index("dp")
    shard_count = lax.axis_size("dp")
    slice_dims = (0, 0, 0, 0, 0, 0, 1, 0, 0, 0, 0, 1, 0)
    shares = tuple(
        (
            lax.dynamic_slice_in_dim(
                total_grad,
                shard_place * (total_grad.shape[dim_index] // shard_count),
                total_grad.shape[dim_index] // shard_count,
                dim_index,
            )
            for total_grad, dim_index in zip(totals, slice_dims)
        )
    )
    return (
        layer_out,
        tokens_grad,
        shares[0],
        shares[1],
        shares[2],
        shares[3],
        shares[4],
        shares[5],
        shares[6],
        shares[7],
        shares[8],
        shares[9],
        shares[10],
        shares[11],
        shares[12],
    )


def solution(mesh):
    placed = (
        P(("dp", "context"), None),
        P("dp", None),
        P("dp"),
        P("dp", "tensor"),
        P("dp", None),
        P("dp", None),
        P("dp"),
        P("dp"),
        P("tensor", "dp"),
        P("dp"),
        P("dp"),
        P("dp", "tensor"),
        P("dp", "tensor"),
        P("tensor", "dp"),
        P("dp"),
        P(("dp", "context"), None),
    )
    return jax.shard_map(
        local,
        mesh=mesh,
        in_specs=placed,
        out_specs=(
            P(("dp", "context"), None),
            P(("dp", "context"), None),
            P("dp"),
            P("dp", "tensor"),
            P("dp", None),
            P("dp", None),
            P("dp"),
            P("dp"),
            P("tensor", "dp"),
            P("dp"),
            P("dp"),
            P("dp", "tensor"),
            P("dp", "tensor"),
            P("tensor", "dp"),
            P("dp"),
        ),
        check_vma=False,
    )
```

profile of v0, /device:TPU:0, one launch (start us, length us, event | category | flops | bytes accessed | tf_op | source)
XLA Modules:
  0.0 614.9 jit_solution(17788061807862818543)
XLA Ops:
  12.6 6.5 %all-reduce.11 = (bf16[640]{0:T(1024)(128)(2,1)S(1)}, bf16[640]{0:T(1024)(128)(2,1)S(1)}, bf16[640]{0:T(1024)(128)(2,1)S(1)}, bf16[640]{0:T(1024)(128)(2,1)}) all-reduce(bf16[640]{0:T(1024)(128)(2,1)S(1)} %dynamic-update-slice.2, bf16[640]{0:T(1024)(128)(2,1)S(1)} %dynamic-update-slice.1, ...), channel_id=1, replica_groups=mesh['dp'=2,'context'=4,'tensor'=4] {'dp'}, use_global_device_ids=true, to_apply=%add.6 | all-reduce | flops 2560 | bytes 10240
  20.6 6.4 %all_gather.40 = bf16[640,256]{1,0:T(8,128)(2,1)S(1)} all-gather(bf16[320,256]{1,0:T(8,128)(2,1)} %param.21), channel_id=1, replica_groups=mesh['dp'=2,'context'=4,'tensor'=4] {'dp'}, dimensions={0}, use_global_device_ids=true | all-gather | bytes 491520 | tf_op jit(solution)/shard_map/all_gather | solution.py:112
  29.5 4.0 collective-permute-start.3
  33.8 4.2 all-gather
  38.1 6.0 all_gather.41
  47.3 3.5 collective-permute-start
  50.8 4.2 all-gather.1
  55.6 6.0 all_gather.43
  61.6 6.0 all_gather.45
  71.4 3.5 collective-permute-start.4
  74.9 2.0 collective-permute-start.1
  78.0 6.2 %collective-permute-done.4 = bf16[768,256]{1,0:T(8,128)(2,1)S(1)} collective-permute-done((bf16[768,256]{1,0:T(8,128)(2,1)S(1)}, bf16[768,256]{1,0:T(8,128)(2,1)S(1)}, u32[]{:S(2)}, u32[]{:S(2)}) %collective-permute-start.4) | collective-permute-done | bytes 393248 | tf_op jit(solution)/shard_map/ppermute | solution.py:20
  84.3 4.4 collective-permute-start.5
  88.7 3.4 collective-permute-done.1
  92.1 4.6 collective-permute-start.2
  97.8 3.9 collective-permute-done.2
  109.4 9.3 %all_gather.48 = bf16[640,512]{1,0:T(8,128)(2,1)} all-gather(bf16[320,512]{1,0:T(8,128)(2,1)} %param.27), channel_id=1, replica_groups=mesh['dp'=2,'context'=4,'tensor'=4] {'dp'}, dimensions={0}, use_global_device_ids=true | all-gather | bytes 983040 | tf_op jit(solution)/shard_map/all_gather | solution.py:120
  118.7 9.2 %all_gather.49 = bf16[640,512]{1,0:T(8,128)(2,1)} all-gather(bf16[320,512]{1,0:T(8,128)(2,1)} %param.28), channel_id=1, replica_groups=mesh['dp'=2,'context'=4,'tensor'=4] {'dp'}, dimensions={0}, use_global_device_ids=true | all-gather | bytes 983040 | tf_op jit(solution)/shard_map/all_gather | solution.py:121
  127.9 7.8 %all_gather.50 = bf16[512,640]{0,1:T(8,128)(2,1)} all-gather(bf16[512,320]{0,1:T(8,128)(2,1)S(1)} %copy-done.67), channel_id=1, replica_groups=mesh['dp'=2,'context'=4,'tensor'=4] {'dp'}, dimensions={1}, use_global_device_ids=true | all-gather | bytes 983040 | tf_op jit(solution)/shard_map/all_gather | solution.py:122
  135.8 9.5 %all-reduce.18.cloned.1.call-done = bf16[768,640]{1,0:T(8,128)(2,1)} async-done(((bf16[768,640]{1,0:T(8,128)(2,1)}), bf16[768,640]{1,0:T(8,128)(2,1)}) %all-reduce.18.cloned.1.call-update) | async-done | bytes 983056 | tf_op jit(solution)/shard_map/psum | solution.py:202
  147.4 1.9 multiply_reduce_fusion
  152.6 2.2 multiply_convert_fusion.2
  155.7 1.8 convolution_convert_fusion.2
  158.8 34.7 %all-reduce.20.cloned.1.call-done = bf16[768,640]{1,0:T(8,128)(2,1)} async-done(((bf16[768,640]{1,0:T(8,128)(2,1)}), bf16[768,640]{1,0:T(8,128)(2,1)}) %all-reduce.20.cloned.1.call-update) | async-done | bytes 983056 | tf_op jit(solution)/shard_map/psum | solution.py:217
  195.2 3.3 fusion.27
  200.2 1.8 multiply_convert_fusion.1
  205.6 3.3 fusion.158
  208.9 32.5 %all-reduce.22.cloned.1.call-done = bf16[768,640]{1,0:T(8,128)(2,1)} async-done(((bf16[768,640]{1,0:T(8,128)(2,1)}), bf16[768,640]{1,0:T(8,128)(2,1)}) %all-reduce.22.cloned.1.call-update) | async-done | bytes 983056 | tf_op jit(solution)/shard_map/psum | solution.py:231
  241.4 3.5 fusion.26
  245.0 4.3 fusion.24
  259.5 2.4 fusion.3
  262.0 2.1 fusion.60
  273.2 6.3 %collective-permute-done.9 = bf16[768,256]{1,0:T(8,128)(2,1)S(1)} collective-permute-done((bf16[768,256]{1,0:T(8,128)(2,1)S(1)}, bf16[768,256]{1,0:T(8,128)(2,1)S(1)}, u32[]{:S(2)}, u32[]{:S(2)}) %collective-permute-start.9) | collective-permute-done | bytes 393248 | tf_op jit(solution)/shard_map/ppermute | solution.py:20
  281.4 6.6 %collective-permute-done.6 = bf16[768,256]{0,1:T(8,128)(2,1)S(1)} collective-permute-done((bf16[768,256]{0,1:T(8,128)(2,1)S(1)}, bf16[768,256]{0,1:T(8,128)(2,1)S(1)}, u32[]{:S(2)}, u32[]{:S(2)}) %collective-permute-start.6) | collective-permute-done | bytes 393248 | tf_op jit(solution)/shard_map/ppermute | solution.py:20
  290.0 6.4 %collective-permute-done.10 = bf16[768,256]{1,0:T(8,128)(2,1)S(1)} collective-permute-done((bf16[768,256]{1,0:T(8,128)(2,1)S(1)}, bf16[768,256]{1,0:T(8,128)(2,1)S(1)}, u32[]{:S(2)}, u32[]{:S(2)}) %collective-permute-start.10) | collective-permute-done | bytes 393248 | tf_op jit(solution)/shard_map/ppermute | solution.py:20
  297.8 7.0 %collective-permute-done.7 = bf16[768,256]{0,1:T(8,128)(2,1)S(1)} collective-permute-done((bf16[768,256]{0,1:T(8,128)(2,1)S(1)}, bf16[768,256]{0,1:T(8,128)(2,1)S(1)}, u32[]{:S(2)}, u32[]{:S(2)}) %collective-permute-start.7) | collective-permute-done | bytes 393248 | tf_op jit(solution)/shard_map/ppermute | solution.py:20
  307.7 5.5 collective-permute-done.11
  314.1 5.6 collective-permute-done.8
  320.6 2.9 fusion.157
  323.6 1.8 fusion.156
  328.2 38.9 %all-reduce.26.cloned.1.call-done = (bf16[768,256]{0,1:T(8,128)(2,1)}, bf16[768,640]{1,0:T(8,128)(2,1)}, bf16[768,256]{1,0:T(8,128)(2,1)}) async-done(((bf16[768,256]{0,1:T(8,128)(2,1)}, bf16[768,640]{1,0:T(8,128)(2,1)}, bf16[768,256]{1,0:T(8,128)(2,1)}), (bf16[768,256]{0,1:T(8,128)(2,1)}, bf16[768,640]{1,0:T(8,128)(2,1)}, bf16[768,256]{1,0:T(8,128)(2,1)})) %all-reduce.26.cloned.1.call-update) | async-done | bytes 1769488 | tf_op jit(solution)/shard_map/psum | solution.py:294
  373.3 5.9 psum.150
  379.8 3.7 fusion.21
  383.5 40.0 %all-reduce.8 = (f32[640]{0:T(1024)S(1)}, f32[256]{0:T(256)S(1)}, f32[256]{0:T(256)S(1)}, f32[640]{0:T(1024)S(1)}, f32[640]{0:T(1024)S(1)}, /*index=5*/f32[640]{0:T(1024)S(1)}) all-reduce(f32[640]{0:T(1024)S(1)} %get-tuple-element.19, bf16[256]{0:T(256)(128)(2,1)S(1)} %psum.150, ...), channel_id=1, replica_groups=mesh['dp'=2,'context'=4,'tensor'=4] {'dp','context'}, use_global_device_ids=true, to_apply=%region_37.38 | all-reduce | flops 3072 | bytes 24064 | tf_op jit(solution)/shard_map/psum | solution.py:315
  427.3 3.3 fusion.30
  430.6 168.5 %all-reduce.24.cloned.1.call-done = (f32[640,256]{1,0:T(8,128)}, f32[640,256]{1,0:T(8,128)}, f32[640,256]{1,0:T(8,128)}, f32[256,640]{0,1:T(8,128)}, f32[640,512...) async-done(((f32[640,256]{1,0:T(8,128)}, f32[640,256]{1,0:T(8,128)}, f32[640,256]{1,0:T(8,128)}, f32[256,640]{0,1:T(8,128)}, f32[640,512]{1,0:T(8,128)}, ...) | async-done | bytes 6553616 | tf_op jit(solution)/shard_map/psum | solution.py:315
  599.1 1.9 constant_dynamic-slice_fusion.5
  602.7 1.8 constant_dynamic-slice_fusion.3
  (376 shorter events, 87.8 us)
Async XLA Ops:
  7.2 138.0 %all-reduce.18.cloned.1.call-start = ((), (), s32[]{:S(2)}) async-start(), calls=%async_computation | async-start | bytes 1966080 | tf_op jit(solution)/shard_map/psum | solution.py:202
  19.0 48.6 %copy-start.87 = (f32[640]{0:T(1024)}, f32[640]{0:T(1024)S(1)}, u32[]{:S(2)}) copy-start(f32[640]{0:T(1024)S(1)} %convert_element_type.203) | copy-start | bytes 7684
  19.0 14.5 %copy-start.116 = (s32[1,2]{1,0:T(1,128)S(1)}, s32[1,2]{1,0:T(1,128)}, u32[]{:S(2)}) copy-start(s32[1,2]{1,0:T(1,128)} %param.17) | copy-start | bytes 28
  19.1 14.7 %copy-start.117 = (bf16[128]{0:T(256)(128)(2,1)S(1)}, bf16[128]{0:T(256)(128)(2,1)}, u32[]{:S(2)}) copy-start(bf16[128]{0:T(256)(128)(2,1)} %param.23) | copy-start | bytes 772
  19.1 19.1 %copy-start.73 = (bf16[320,256]{1,0:T(8,128)(2,1)S(1)}, bf16[320,256]{1,0:T(8,128)(2,1)}, u32[]{:S(2)}) copy-start(bf16[320,256]{1,0:T(8,128)(2,1)} %param.20) | copy-start | bytes 491524
  20.6 24.2 %copy-start.91 = (f32[768]{0:T(1024)}, f32[768]{0:T(1024)S(1)}, u32[]{:S(2)}) copy-start(f32[768]{0:T(1024)S(1)} %fusion.35) | copy-start | bytes 9220
  20.6 23.6 %copy-start.6 = (bf16[768,640]{1,0:T(8,128)(2,1)S(1)}, bf16[768,640]{1,0:T(8,128)(2,1)}, u32[]{:S(2)}) copy-start(bf16[768,640]{1,0:T(8,128)(2,1)} %param.16) | copy-start | bytes 2949124
  20.6 47.0 %copy-start.89 = (f32[768]{0:T(1024)}, f32[768]{0:T(1024)S(1)}, u32[]{:S(2)}) copy-start(f32[768]{0:T(1024)S(1)} %fusion.124) | copy-start | bytes 9220
  29.5 16.0 %copy-start.39 = (bf16[768,256]{1,0:T(8,128)(2,1)}, bf16[768,256]{1,0:T(8,128)(2,1)S(1)}, u32[]{:S(2)}) copy-start(bf16[768,256]{1,0:T(8,128)(2,1)S(1)} %convolution_convert_fusion.5) | copy-start | bytes 1179652
  29.5 41.9 %collective-permute-start.3 = (bf16[768,256]{1,0:T(8,128)(2,1)S(1)}, bf16[768,256]{1,0:T(8,128)(2,1)S(1)}, u32[]{:S(2)}, u32[]{:S(2)}) collective-permute-start(bf16[768,256]{1,0:T(8,128)(2,1)S(1)} %convolution_convert_fusion.5), channel_id=1, source_target_pairs={{0,4},{4,8},{8,12},{1,5},{5,9},{9,13},{2,6},{6,10},{10,14},{3,7},{... | collective-permute-start | bytes 1179656 | tf_op jit(solution)/shard_map/ppermute | solution.py:20
  33.5 35.0 %copy-start.114 = (f32[128]{0:T(128)}, f32[128]{0:T(128)S(1)}, u32[]{:S(2)}) copy-start(f32[128]{0:T(128)S(1)} %multiply_exponential_fusion) | copy-start | bytes 1540
  33.5 12.0 %copy-start.112 = (s32[768]{0:T(1024)}, s32[768]{0:T(1024)S(1)}, u32[]{:S(2)}) copy-start(s32[768]{0:T(1024)S(1)} %get-tuple-element.90) | copy-start | bytes 9220
  33.6 43.3 %copy-start.108 = (s32[768]{0:T(1024)}, s32[768]{0:T(1024)S(1)}, u32[]{:S(2)}) copy-start(s32[768]{0:T(1024)S(1)} %get-tuple-element.88) | copy-start | bytes 9220
  44.8 16.8 %copy-start.17 = (f32[768,256]{0,1:T(8,128)}, f32[768,256]{0,1:T(8,128)S(1)}, u32[]{:S(2)}) copy-start(f32[768,256]{0,1:T(8,128)S(1)} %get-tuple-element.73) | copy-start | bytes 2359300
  44.9 16.7 %copy-start.83 = (f32[768]{0:T(1024)}, f32[768]{0:T(1024)S(1)}, u32[]{:S(2)}) copy-start(f32[768]{0:T(1024)S(1)} %fusion.125) | copy-start | bytes 9220
  45.4 16.2 %copy-start.75 = (bf16[256,320]{0,1:T(8,128)(2,1)S(1)}, bf16[256,320]{0,1:T(8,128)(2,1)}, u32[]{:S(2)}) copy-start(bf16[256,320]{0,1:T(8,128)(2,1)} %param.24) | copy-start | bytes 491524
  47.2 23.0 %copy-start.31 = (bf16[768,128]{0,1:T(8,128)(2,1)}, bf16[768,128]{0,1:T(8,128)(2,1)S(1)}, u32[]{:S(2)}) copy-start(bf16[768,128]{0,1:T(8,128)(2,1)S(1)} %get-tuple-element.67) | copy-start | bytes 589828
  47.3 27.6 %collective-permute-start = (bf16[768,256]{0,1:T(8,128)(2,1)S(1)}, bf16[768,256]{0,1:T(8,128)(2,1)S(1)}, u32[]{:S(2)}, u32[]{:S(2)}) collective-permute-start(bf16[768,256]{0,1:T(8,128)(2,1)S(1)} %pad_maximum_fusion), channel_id=1, source_target_pairs={{0,4},{4,8},{8,12},{1,5},{5,9},{9,13},{2,6},{6,10},{10,14},{3,7},{... | collective-permute-start | bytes 1179656 | tf_op jit(solution)/shard_map/ppermute | solution.py:20
  55.0 13.5 %copy-start.100 = (f32[2,1,128]{2,1,0:T(1,128)}, f32[2,1,128]{2,1,0:T(1,128)S(1)}, u32[]{:S(2)}) copy-start(f32[2,1,128]{2,1,0:T(1,128)S(1)} %convert_element_type.259) | copy-start | bytes 3076
  67.6 39.3 %copy-start.27 = (bf16[256,640]{0,1:T(8,128)(2,1)}, bf16[256,640]{0,1:T(8,128)(2,1)S(1)}, u32[]{:S(2)}) copy-start(bf16[256,640]{0,1:T(8,128)(2,1)S(1)} %all_gather.45) | copy-start | bytes 983044
  70.2 31.6 %copy-start.68 = (bf16[768,128]{0,1:T(8,128)(2,1)}, bf16[768,128]{0,1:T(8,128)(2,1)S(1)}, u32[]{:S(2)}) copy-start(bf16[768,128]{0,1:T(8,128)(2,1)S(1)} %get-tuple-element.64) | copy-start | bytes 589828
  70.2 31.6 %copy-start.70 = (bf16[768,128]{0,1:T(8,128)(2,1)}, bf16[768,128]{0,1:T(8,128)(2,1)S(1)}, u32[]{:S(2)}) copy-start(bf16[768,128]{0,1:T(8,128)(2,1)S(1)} %get-tuple-element.65) | copy-start | bytes 589828
  71.0 32.7 %copy-start = (f32[1,768,768]{1,2,0:T(8,128)}, f32[1,768,768]{1,2,0:T(8,128)S(1)}, u32[]{:S(2)}) copy-start(f32[1,768,768]{1,2,0:T(8,128)S(1)} %get-tuple-element.83) | copy-start | bytes 7077892
  71.4 12.9 %collective-permute-start.4 = (bf16[768,256]{1,0:T(8,128)(2,1)S(1)}, bf16[768,256]{1,0:T(8,128)(2,1)S(1)}, u32[]{:S(2)}, u32[]{:S(2)}) collective-permute-start(bf16[768,256]{1,0:T(8,128)(2,1)S(1)} %collective-permute-done.3), channel_id=1, source_target_pairs={{0,4},{4,8},{8,12},{1,5},{5,9},{9,13},{2,6},{6,10},{10,14},{3,7},{... | collective-permute-start | bytes 1179656 | tf_op jit(solution)/shard_map/ppermute | solution.py:20
  74.9 17.2 %collective-permute-start.1 = (bf16[768,256]{0,1:T(8,128)(2,1)S(1)}, bf16[768,256]{0,1:T(8,128)(2,1)S(1)}, u32[]{:S(2)}, u32[]{:S(2)}) collective-permute-start(bf16[768,256]{0,1:T(8,128)(2,1)S(1)} %collective-permute-done), channel_id=1, source_target_pairs={{0,4},{4,8},{8,12},{1,5},{5,9},{9,13},{2,6},{6,10},{10,14},{3,7},{... | collective-permute-start | bytes 1179656 | tf_op jit(solution)/shard_map/ppermute | solution.py:20
  77.6 27.5 %copy-start.2 = (f32[1,768,768]{1,2,0:T(8,128)}, f32[1,768,768]{1,2,0:T(8,128)S(1)}, u32[]{:S(2)}) copy-start(f32[1,768,768]{1,2,0:T(8,128)S(1)} %get-tuple-element.81) | copy-start | bytes 7077892
  77.6 19.1 %copy-start.109 = (s32[768]{0:T(1024)S(1)}, s32[768]{0:T(1024)}, u32[]{:S(2)}) copy-start(s32[768]{0:T(1024)} %copy-done.108) | copy-start | bytes 9220
  77.7 19.1 %copy-start.113 = (s32[768]{0:T(1024)S(1)}, s32[768]{0:T(1024)}, u32[]{:S(2)}) copy-start(s32[768]{0:T(1024)} %copy-done.112) | copy-start | bytes 9220
  84.3 21.5 %copy-start.33 = (bf16[768,256]{1,0:T(8,128)(2,1)}, bf16[768,256]{1,0:T(8,128)(2,1)S(1)}, u32[]{:S(2)}) copy-start(bf16[768,256]{1,0:T(8,128)(2,1)S(1)} %collective-permute-done.4) | copy-start | bytes 1179652
  84.3 22.0 %collective-permute-start.5 = (bf16[768,256]{1,0:T(8,128)(2,1)S(1)}, bf16[768,256]{1,0:T(8,128)(2,1)S(1)}, u32[]{:S(2)}, u32[]{:S(2)}) collective-permute-start(bf16[768,256]{1,0:T(8,128)(2,1)S(1)} %collective-permute-done.4), channel_id=1, source_target_pairs={{0,4},{4,8},{8,12},{1,5},{5,9},{9,13},{2,6},{6,10},{10,14},{3,7},{... | collective-permute-start | bytes 1179656 | tf_op jit(solution)/shard_map/ppermute | solution.py:20
  92.1 9.7 %collective-permute-start.2 = (bf16[768,256]{0,1:T(8,128)(2,1)S(1)}, bf16[768,256]{0,1:T(8,128)(2,1)S(1)}, u32[]{:S(2)}, u32[]{:S(2)}) collective-permute-start(bf16[768,256]{0,1:T(8,128)(2,1)S(1)} %collective-permute-done.1), channel_id=1, source_target_pairs={{0,4},{4,8},{8,12},{1,5},{5,9},{9,13},{2,6},{6,10},{10,14},{3,7},{... | collective-permute-start | bytes 1179656 | tf_op jit(solution)/shard_map/ppermute | solution.py:20
  109.3 84.2 %all-reduce.20.cloned.1.call-start = ((), (), s32[]{:S(2)}) async-start(), calls=%async_computation.1 | async-start | bytes 1966080 | tf_op jit(solution)/shard_map/psum | solution.py:217
  109.3 18.6 %copy-start.67 = (bf16[512,320]{0,1:T(8,128)(2,1)S(1)}, bf16[512,320]{0,1:T(8,128)(2,1)}, u32[]{:S(2)}) copy-start(bf16[512,320]{0,1:T(8,128)(2,1)} %param.29) | copy-start | bytes 983044
  157.5 83.9 %all-reduce.22.cloned.1.call-start = ((), (), s32[]{:S(2)}) async-start(), calls=%async_computation.2 | async-start | bytes 1966080 | tf_op jit(solution)/shard_map/psum | solution.py:231
  205.4 161.7 %all-reduce.26.cloned.1.call-start = ((), (), s32[]{:S(2)}) async-start(), calls=%async_computation.4 | async-start | bytes 3538944 | tf_op jit(solution)/shard_map/psum | solution.py:294
  265.6 13.9 %collective-permute-start.9 = (bf16[768,256]{1,0:T(8,128)(2,1)S(1)}, bf16[768,256]{1,0:T(8,128)(2,1)S(1)}, u32[]{:S(2)}, u32[]{:S(2)}) collective-permute-start(bf16[768,256]{1,0:T(8,128)(2,1)S(1)} %convolution_convert_fusion.3), channel_id=1, source_target_pairs={{4,0},{8,4},{12,8},{5,1},{9,5},{13,9},{6,2},{10,6},{14,10},{7,3},{... | collective-permute-start | bytes 1179656 | tf_op jit(solution)/shard_map/ppermute | solution.py:20
  271.3 16.7 %collective-permute-start.6 = (bf16[768,256]{0,1:T(8,128)(2,1)S(1)}, bf16[768,256]{0,1:T(8,128)(2,1)S(1)}, u32[]{:S(2)}, u32[]{:S(2)}) collective-permute-start(bf16[768,256]{0,1:T(8,128)(2,1)S(1)} %fusion.53), channel_id=1, source_target_pairs={{4,0},{8,4},{12,8},{5,1},{9,5},{13,9},{6,2},{10,6},{14,10},{7,3},{... | collective-permute-start | bytes 1179656 | tf_op jit(solution)/shard_map/ppermute | solution.py:20
  280.1 16.3 %collective-permute-start.10 = (bf16[768,256]{1,0:T(8,128)(2,1)S(1)}, bf16[768,256]{1,0:T(8,128)(2,1)S(1)}, u32[]{:S(2)}, u32[]{:S(2)}) collective-permute-start(bf16[768,256]{1,0:T(8,128)(2,1)S(1)} %add_convert_fusion.3), channel_id=1, source_target_pairs={{4,0},{8,4},{12,8},{5,1},{9,5},{13,9},{6,2},{10,6},{14,10},{7,3},{... | collective-permute-start | bytes 1179656 | tf_op jit(solution)/shard_map/ppermute | solution.py:20
  288.5 16.3 %collective-permute-start.7 = (bf16[768,256]{0,1:T(8,128)(2,1)S(1)}, bf16[768,256]{0,1:T(8,128)(2,1)S(1)}, u32[]{:S(2)}, u32[]{:S(2)}) collective-permute-start(bf16[768,256]{0,1:T(8,128)(2,1)S(1)} %add_convert_fusion.6), channel_id=1, source_target_pairs={{4,0},{8,4},{12,8},{5,1},{9,5},{13,9},{6,2},{10,6},{14,10},{7,3},{... | collective-permute-start | bytes 1179656 | tf_op jit(solution)/shard_map/ppermute | solution.py:20
  290.0 16.2 %copy-start.48 = (bf16[640,256]{1,0:T(8,128)(2,1)S(1)}, bf16[640,256]{1,0:T(8,128)(2,1)}, u32[]{:S(2)}) copy-start(bf16[640,256]{1,0:T(8,128)(2,1)} %copy-done.47) | copy-start | bytes 983044
  296.5 16.8 %collective-permute-start.11 = (bf16[768,256]{1,0:T(8,128)(2,1)S(1)}, bf16[768,256]{1,0:T(8,128)(2,1)S(1)}, u32[]{:S(2)}, u32[]{:S(2)}) collective-permute-start(bf16[768,256]{1,0:T(8,128)(2,1)S(1)} %add_convert_fusion.2), channel_id=1, source_target_pairs={{4,0},{8,4},{12,8},{5,1},{9,5},{13,9},{6,2},{10,6},{14,10},{7,3},{... | collective-permute-start | bytes 1179656 | tf_op jit(solution)/shard_map/ppermute | solution.py:20
  304.9 14.8 %collective-permute-start.8 = (bf16[768,256]{0,1:T(8,128)(2,1)S(1)}, bf16[768,256]{0,1:T(8,128)(2,1)S(1)}, u32[]{:S(2)}, u32[]{:S(2)}) collective-permute-start(bf16[768,256]{0,1:T(8,128)(2,1)S(1)} %add_convert_fusion.5), channel_id=1, source_target_pairs={{4,0},{8,4},{12,8},{5,1},{9,5},{13,9},{6,2},{10,6},{14,10},{7,3},{... | collective-permute-start | bytes 1179656 | tf_op jit(solution)/shard_map/ppermute | solution.py:20
  320.6 278.5 %all-reduce.24.cloned.1.call-start = ((), (), s32[]{:S(2)}) async-start(), calls=%async_computation.3 | async-start | bytes 13107200 | tf_op jit(solution)/shard_map/psum | solution.py:315
  328.2 41.6 %copy-start.18 = (f32[768,256]{0,1:T(8,128)S(1)}, f32[768,256]{0,1:T(8,128)}, u32[]{:S(2)}) copy-start(f32[768,256]{0,1:T(8,128)} %copy-done.17) | copy-start | bytes 2359300
  328.2 41.7 %copy-start.84 = (f32[768]{0:T(1024)S(1)}, f32[768]{0:T(1024)}, u32[]{:S(2)}) copy-start(f32[768]{0:T(1024)} %copy-done.83) | copy-start | bytes 9220
  328.2 41.7 %copy-start.99 = (f32[2,1,128]{2,1,0:T(1,128)S(1)}, f32[2,1,128]{2,1,0:T(1,128)}, u32[]{:S(2)}) copy-start(f32[2,1,128]{2,1,0:T(1,128)} %copy-done.98) | copy-start | bytes 3076
  379.8 47.5 %copy-start.92 = (f32[768]{0:T(1024)S(1)}, f32[768]{0:T(1024)}, u32[]{:S(2)}) copy-start(f32[768]{0:T(1024)} %copy-done.91) | copy-start | bytes 9220
  379.8 47.5 %copy-start.10 = (f32[768,640]{1,0:T(8,128)S(1)}, f32[768,640]{1,0:T(8,128)}, u32[]{:S(2)}) copy-start(f32[768,640]{1,0:T(8,128)} %copy-done.9) | copy-start | bytes 5898244
  (90 other events, 276.1 us)
Sparse Core Ops, SparseCore 0:
  109.4 35.7 all-reduce.17
  157.6 35.8 all-reduce.19
  205.5 35.8 all-reduce.21
  320.7 46.3 all-reduce.25
  373.4 225.6 all-reduce.23
where the time goes:
time: 623 us; the launch traced here: 615 us
  waiting for transfers between devices  335 us (54%)
  blocking collectives  112 us (18%)
  matrix products  48.5 us (8%)
  other arithmetic  39.9 us (6%)
  local copies, waits for them, and re-layouts  32.8 us (5%)
  starting transfers between devices  30.3 us (5%)
  between operations  16.5 us (3%)
    psum x1, waiting for transfers between devices, local(): lax.psum((grad_ginput, grad_wquery, grad_wkey, grad_wvalue, grad_gquery,...  168 us
    ppermute x12, waiting for transfers between devices, passed_along(): return lax.ppermute(array, axis, pairs)  51.1 us
    psum x1, blocking collectives, local(): lax.psum((grad_ginput, grad_wquery, grad_wkey, grad_wvalue, grad_gquery,...  40 us
    psum x1, waiting for transfers between devices, local(): lax.psum(carried[0].astype(jnp.bfloat16), 'tensor').astype(jnp.float32)  38.9 us
    psum x1, waiting for transfers between devices, local(): lax.psum(product(hidden, w_down).astype(jnp.bfloat16), 'tensor')  34.7 us
    psum x1, waiting for transfers between devices, local(): lax.psum((product_rt(grad_gate, w_gate) + product_rt(grad_up, w_up)).asty...  32.5 us
    ppermute x12, starting transfers between devices, passed_along(): return lax.ppermute(array, axis, pairs)  29.9 us
    unnamed x251, local copies, waits for them, and re-layouts  20.2 us
  transfers between devices with their start and end apart: 17, of which 14 were waited for; matrix products, arithmetic and copies ran while one was open for 7% of the time, Pallas kernels for 0%

commit v1 on v0

v1 whole, which is shorter than its diff:
```python
import math

import jax
import jax.numpy as jnp
from jax import lax
from jax.sharding import PartitionSpec as P

HD = 256
LMAX = 2048
EPS = 1e-06
SCALE = 0.0625

BF = jnp.bfloat16
F32 = jnp.float32


def product(left_side, right_side):
    return jnp.dot(left_side, right_side, preferred_element_type=F32)


def product_lt(left_side, right_side):
    return lax.dot_general(
        left_side, right_side, (((0,), (0,)), ((), ())), preferred_element_type=F32
    )


def product_rt(left_side, right_side):
    return lax.dot_general(
        left_side, right_side, (((1,), (1,)), ((), ())), preferred_element_type=F32
    )


def low(values):
    return lax.reduce_precision(values, 8, 7).astype(BF)


def over_core(array):
    devices = lax.axis_size("tensor")
    return lax.ppermute(array, "tensor", [(i, i ^ 1) for i in range(devices)])


def over_pairs(array):
    devices = lax.axis_size("tensor")
    return lax.ppermute(array, "tensor", [(i, i ^ 2) for i in range(devices)])


def over_context(array, by):
    devices = lax.axis_size("context")
    pairs = [(i, i + by) for i in range(devices) if 0 <= i + by < devices]
    return lax.ppermute(array, "context", pairs)


def after(array, earlier):
    return lax.optimization_barrier((array, earlier))[0]


def ordered(place, mine, other):
    return jnp.where(
        place == 0,
        jnp.concatenate([mine, other], axis=0),
        jnp.concatenate([other, mine], axis=0),
    )


def pairs_sum(partial):
    short = low(partial)
    return short.astype(F32) + over_pairs(short).astype(F32)


def dp_gathered(array):
    if lax.axis_size("dp") == 2:
        other = lax.ppermute(array, "dp", [(0, 1), (1, 0)])
        return ordered(lax.axis_index("dp"), array, other)
    return lax.all_gather(array, "dp", axis=0, tiled=True)


def dp_scattered(total):
    if lax.axis_size("dp") == 2:
        place = lax.axis_index("dp")
        rows = total.shape[0] // 2
        keep = lax.dynamic_slice_in_dim(total, place * rows, rows, 0)
        send = lax.dynamic_slice_in_dim(total, (1 - place) * rows, rows, 0)
        return keep.astype(F32) + lax.ppermute(low(send), "dp", [(0, 1), (1, 0)]).astype(F32)
    return lax.psum_scatter(low(total), "dp", scatter_dimension=0, tiled=True).astype(F32)


def context_sum(total):
    if lax.axis_size("context") != 4:
        return lax.psum(total, "context")
    place = lax.axis_index("context")
    near, far = place % 2, place // 2
    rows = total.shape[0] // 2
    keep = lax.dynamic_slice_in_dim(total, near * rows, rows, 0)
    send = lax.dynamic_slice_in_dim(total, (1 - near) * rows, rows, 0)
    by_near = [(i, i ^ 1) for i in range(4)]
    by_far = [(i, i ^ 2) for i in range(4)]
    part = keep + lax.ppermute(low(send), "context", by_near).astype(F32)
    rows = rows // 2
    keep = lax.dynamic_slice_in_dim(part, far * rows, rows, 0)
    send = lax.dynamic_slice_in_dim(part, (1 - far) * rows, rows, 0)
    part = low(keep + lax.ppermute(low(send), "context", by_far).astype(F32))
    part = ordered(far, part, lax.ppermute(part, "context", by_far))
    return ordered(near, part, lax.ppermute(part, "context", by_near)).astype(F32)


def context_sum_small(total):
    if lax.axis_size("context") != 4:
        return lax.psum(total, "context")
    for bit in (1, 2):
        short = low(total)
        other = lax.ppermute(short, "context", [(i, i ^ bit) for i in range(4)])
        total = short.astype(F32) + other.astype(F32)
    return total


def normed_of(values):
    inverse = lax.rsqrt(jnp.mean(values * values, axis=-1, keepdims=True) + EPS)
    return values * inverse, inverse


def norm_back(grad, gain, unit, inverse):
    scaled = grad * gain
    return inverse * (scaled - unit * jnp.mean(scaled * unit, axis=-1, keepdims=True))


def turned(values, cosines, sines):
    half_width = values.shape[-1] // 2
    first_half = values[..., :half_width]
    second_half = values[..., half_width:]
    return jnp.concatenate(
        [first_half * cosines - second_half * sines, second_half * cosines + first_half * sines],
        axis=-1,
    )


def local(
    tokens,
    seq_lengths,
    input_gain,
    query_weight,
    key_weight,
    value_weight,
    query_gain,
    key_gain,
    output_weight,
    attention_gain,
    prefeed_gain,
    gate_weight,
    up_weight,
    down_weight,
    feed_gain,
    cotangent,
):
    block_rows = tokens.shape[0]
    rows = block_rows // 2
    width = tokens.shape[1]
    context_place = lax.axis_index("context")
    core = lax.axis_index("tensor") % 2
    pair = lax.axis_index("tensor") // 2
    reach = min(lax.axis_size("context") - 1, (LMAX - 2) // block_rows + 1)
    dp_count = lax.axis_size("dp")
    shard = width // dp_count
    feed_width = gate_weight.shape[1]

    gains = jnp.concatenate(
        [input_gain, attention_gain, prefeed_gain, feed_gain, query_gain, key_gain]
    ).reshape(1, -1)
    gain_parts = lax.all_gather(gains, "dp", axis=0, tiled=True)
    kv_pack = jnp.concatenate([key_weight, value_weight], axis=1)
    qo_pack = jnp.concatenate([query_weight, output_weight.T], axis=1)
    feed_pack = jnp.concatenate([gate_weight, up_weight, down_weight.T], axis=1)
    w_kv = dp_gathered(kv_pack)
    w_qo = dp_gathered(after(qo_pack, w_kv))
    w_feed = dp_gathered(after(feed_pack, w_qo))
    w_qo_other = over_core(w_qo)
    w_feed_other = over_core(w_feed)

    def gain_of(first, count):
        return gain_parts[:, first : first + count].reshape(1, -1).astype(F32)

    g_input, g_attention, g_prefeed, g_feed = (gain_of(i * shard, shard) for i in range(4))
    head_shard = HD // dp_count
    g_query, g_key = (gain_of(4 * shard + i * head_shard, head_shard) for i in range(2))

    stream = lax.dynamic_slice_in_dim(tokens, core * rows, rows, 0).astype(F32)
    grad_out = lax.dynamic_slice_in_dim(cotangent, core * rows, rows, 0).astype(F32)
    row_index = (
        context_place * block_rows + core * rows + lax.broadcasted_iota(jnp.int32, (rows, 1), 0)
    )
    start = jnp.zeros_like(row_index)
    begin = jnp.int32(0)
    for number in range(seq_lengths.shape[1]):
        start = jnp.where(row_index >= begin, begin, start)
        begin = begin + seq_lengths[0, number]
    frequency = jnp.exp(
        lax.broadcasted_iota(jnp.int32, (1, HD // 2), 1).astype(F32)
        * (-2.0 * math.log(1000000.0) / HD)
    )
    angles = (row_index - start).astype(F32) * frequency
    cosines, sines = lax.optimization_barrier((jnp.cos(angles), jnp.sin(angles)))
    two_cosines = jnp.concatenate([cosines, cosines], axis=0)
    two_sines = jnp.concatenate([sines, sines], axis=0)

    input_unit, input_inverse = normed_of(stream)
    normed = (input_unit * g_input).astype(BF)

    key_value_raw = product(normed, w_kv)
    key_unit, key_inverse = normed_of(key_value_raw[:, :HD])
    key_own = turned(key_unit * g_key, cosines, sines).astype(BF)
    value_own = key_value_raw[:, HD:].astype(BF)
    blocks = []
    current = (key_own, value_own)
    for step in range(reach + 1):
        if step > 0:
            current = (over_context(current[0], 1), over_context(current[1], 1))
        blocks.append(
            (
                jnp.concatenate([current[0], over_core(current[0])], axis=0),
                jnp.concatenate([current[1], over_core(current[1])], axis=0),
            )
        )

    query_raw = jnp.concatenate(
        [product(normed, w_qo[:, :HD]), product(normed, w_qo_other[:, :HD])], axis=0
    )
    query_unit, query_inverse = normed_of(query_raw)
    query = turned(query_unit * g_query, two_cosines, two_sines).astype(BF)

    two_rows = jnp.concatenate([row_index, row_index], axis=0)
    two_starts = jnp.concatenate([start, start], axis=0)
    within = lax.broadcasted_iota(jnp.int32, (1, rows), 1)
    key_rows = jnp.concatenate([core * rows + within, (1 - core) * rows + within], axis=1)
    kept = []
    mass = jnp.zeros((2 * rows, 1), F32)
    heads_sum = jnp.zeros((2 * rows, HD), F32)
    for step in range(reach + 1):
        key_block, value_block = blocks[step]
        key_index = (context_place - step) * block_rows + key_rows
        allowed = (key_index >= two_starts) & (key_index <= two_rows)
        weights = jnp.where(allowed, jnp.exp(product_rt(query, key_block) * SCALE), 0.0)
        mass = mass + jnp.sum(weights, axis=1, keepdims=True)
        weights = weights.astype(BF)
        heads_sum = heads_sum + product(weights, value_block)
        kept.append(weights)
    inverse_mass = 1.0 / mass
    heads = heads_sum * inverse_mass
    heads_low = heads.astype(BF)
    heads_wide = jnp.concatenate([heads_low[:rows], heads_low[rows:]], axis=1)
    w_output = jnp.concatenate([w_qo[:, HD:], w_qo_other[:, HD:]], axis=1)
    attn_sum = pairs_sum(product_rt(heads_wide, w_output))

    w_gate_up = jnp.concatenate(
        [
            w_feed[:, :feed_width],
            w_feed_other[:, :feed_width],
            w_feed[:, feed_width : 2 * feed_width],
            w_feed_other[:, feed_width : 2 * feed_width],
        ],
        axis=1,
    )
    w_down = jnp.concatenate([w_feed[:, 2 * feed_width :], w_feed_other[:, 2 * feed_width :]], axis=1)
    attn_unit, attn_inverse = normed_of(attn_sum)
    middle = stream + attn_unit * g_attention
    middle_unit, middle_inverse = normed_of(middle)
    normed_feed = (middle_unit * g_prefeed).astype(BF)
    gate_up = product(normed_feed, w_gate_up)
    activation, activation_back = jax.vjp(
        lambda gate_part, up_part: jax.nn.gelu(gate_part, approximate=True) * up_part,
        gate_up[:, : 2 * feed_width],
        gate_up[:, 2 * feed_width :],
    )
    hidden = activation.astype(BF)
    feed_sum = pairs_sum(product_rt(hidden, w_down))
    feed_unit, feed_inverse = normed_of(feed_sum)
    layer_own = low(middle + feed_unit * g_feed)
    layer_out = ordered(core, layer_own, over_core(layer_own))

    grad_gfeed = jnp.sum(grad_out * feed_unit, axis=0, keepdims=True)
    grad_feed = norm_back(grad_out, g_feed, feed_unit, feed_inverse).astype(BF)
    grad_gate_full, grad_up_full = activation_back(product(grad_feed, w_down))
    grad_gate_up = jnp.concatenate([grad_gate_full.astype(BF), grad_up_full.astype(BF)], axis=1)
    grad_normed_feed = pairs_sum(product_rt(grad_gate_up, w_gate_up))

    def shared(total, own, other):
        mine = jnp.concatenate([total[:, a:b] for a, b in own], axis=1)
        theirs = jnp.concatenate([total[:, a:b] for a, b in other], axis=1)
        whole = mine + over_core(low(theirs)).astype(F32)
        return context_sum(dp_scattered(whole))

    total_down = shared(
        product_lt(grad_feed, hidden), [(0, feed_width)], [(feed_width, 2 * feed_width)]
    )
    total_gate_up = shared(
        product_lt(normed_feed, grad_gate_up),
        [(0, feed_width), (2 * feed_width, 3 * feed_width)],
        [(feed_width, 2 * feed_width), (3 * feed_width, 4 * feed_width)],
    )

    grad_gprefeed = jnp.sum(grad_normed_feed * middle_unit, axis=0, keepdims=True)
    grad_middle = grad_out + norm_back(grad_normed_feed, g_prefeed, middle_unit, middle_inverse)
    grad_gattention = jnp.sum(grad_middle * attn_unit, axis=0, keepdims=True)
    grad_attn = norm_back(grad_middle, g_attention, attn_unit, attn_inverse).astype(BF)

    grad_heads_wide = product(grad_attn, w_output)
    grad_heads = jnp.concatenate([grad_heads_wide[:, :HD], grad_heads_wide[:, HD:]], axis=0)
    grad_heads_low = (grad_heads * inverse_mass).astype(BF)
    row_dots = jnp.sum(grad_heads * heads, axis=1, keepdims=True) * inverse_mass
    grad_query = jnp.zeros((2 * rows, HD), F32)
    carried = None
    for step in range(reach, -1, -1):
        key_block, value_block = blocks[step]
        weights = kept[step]
        grad_scores = (
            weights.astype(F32) * (product_rt(grad_heads_low, value_block) - row_dots)
        ).astype(BF)
        grad_query = grad_query + product(grad_scores, key_block)
        value_part = product_lt(weights, grad_heads_low)
        key_part = product_lt(grad_scores, query) * SCALE
        value_sum = value_part[:rows] + over_core(low(value_part[rows:])).astype(F32)
        key_sum = key_part[:rows] + over_core(low(key_part[rows:])).astype(F32)
        if carried is not None:
            value_sum = value_sum + carried[0].astype(F32)
            key_sum = key_sum + carried[1].astype(F32)
        if step > 0:
            carried = (over_context(low(value_sum), -1), over_context(low(key_sum), -1))

    grad_query_turned = turned(grad_query * SCALE, two_cosines, -two_sines)
    grad_gquery = jnp.sum(grad_query_turned * query_unit, axis=0, keepdims=True)
    grad_query_raw = norm_back(grad_query_turned, g_query, query_unit, query_inverse).astype(BF)
    grad_query_wide = jnp.concatenate([grad_query_raw[:rows], grad_query_raw[rows:]], axis=1)
    grad_q_total = product_lt(normed, grad_query_wide)
    grad_o_total = product_lt(grad_attn, heads_wide)
    total_qo = shared(
        jnp.concatenate([grad_q_total, grad_o_total], axis=1),
        [(0, HD), (2 * HD, 3 * HD)],
        [(HD, 2 * HD), (3 * HD, 4 * HD)],
    )

    grad_key_turned = turned(key_sum, cosines, -sines)
    grad_gkey = jnp.sum(grad_key_turned * key_unit, axis=0, keepdims=True)
    grad_key_raw = norm_back(grad_key_turned, g_key, key_unit, key_inverse).astype(BF)
    grad_kv_raw = jnp.concatenate([grad_key_raw, value_sum.astype(BF)], axis=1)
    grad_normed_part = product_rt(
        jnp.concatenate([grad_query_wide, grad_kv_raw], axis=1),
        jnp.concatenate([w_qo[:, :HD], w_qo_other[:, :HD], w_kv], axis=1),
    )
    grad_normed = pairs_sum(grad_normed_part)
    grad_ginput = jnp.sum(grad_normed_part * input_unit, axis=0, keepdims=True)
    tokens_own = grad_middle + norm_back(grad_normed, g_input, input_unit, input_inverse)
    tokens_grad = ordered(core, tokens_own, over_core(tokens_own))

    lanes = 2 * HD

    def spread(vector, count):
        parts = vector.reshape(dp_count, 1, count)
        return jnp.pad(parts, ((0, 0), (0, 0), (0, lanes - count)))

    once = jnp.where(pair == 0, 1.0, 0.0).astype(F32)
    gain_rows = jnp.concatenate(
        [
            spread(grad_ginput, shard),
            spread(grad_gattention * once, shard),
            spread(grad_gprefeed * once, shard),
            spread(grad_gfeed * once, shard),
            spread(grad_gquery, head_shard),
            spread(grad_gkey, head_shard),
            jnp.zeros((dp_count, 10, lanes), F32),
        ],
        axis=1,
    )
    small = jnp.concatenate(
        [product_lt(normed, grad_kv_raw).reshape(dp_count, shard, lanes), gain_rows], axis=1
    ).reshape(dp_count * (shard + 16), lanes)
    columns = lanes // 2
    small = lax.dynamic_slice_in_dim(small, core * columns, columns, 1) + over_core(
        low(lax.dynamic_slice_in_dim(small, (1 - core) * columns, columns, 1))
    ).astype(F32)
    columns = columns // 2
    small = lax.dynamic_slice_in_dim(small, pair * columns, columns, 1) + over_pairs(
        low(lax.dynamic_slice_in_dim(small, (1 - pair) * columns, columns, 1))
    ).astype(F32)
    small = low(context_sum_small(dp_scattered(small)))
    other = over_pairs(small)
    small = jnp.where(
        pair == 0,
        jnp.concatenate([small, other], axis=1),
        jnp.concatenate([other, small], axis=1),
    )
    other = over_core(small)
    small = jnp.where(
        core == 0,
        jnp.concatenate([small, other], axis=1),
        jnp.concatenate([other, small], axis=1),
    ).astype(F32)

    return (
        layer_out,
        tokens_grad,
        small[shard, :shard],
        total_qo[:, :HD],
        small[:shard, :HD],
        small[:shard, HD:],
        small[shard + 4, :head_shard],
        small[shard + 5, :head_shard],
        total_qo[:, HD:].T,
        small[shard + 1, :shard],
        small[shard + 2, :shard],
        total_gate_up[:, :feed_width],
        total_gate_up[:, feed_width:],
        total_down.T,
        small[shard + 3, :shard],
    )


def solution(mesh):
    placed = (
        P(("dp", "context"), None),
        P("dp", None),
        P("dp"),
        P("dp", "tensor"),
        P("dp", None),
        P("dp", None),
        P("dp"),
        P("dp"),
        P("tensor", "dp"),
        P("dp"),
        P("dp"),
        P("dp", "tensor"),
        P("dp", "tensor"),
        P("tensor", "dp"),
        P("dp"),
        P(("dp", "context"), None),
    )
    return jax.shard_map(
        local,
        mesh=mesh,
        in_specs=placed,
        out_specs=(
            P(("dp", "context"), None),
            P(("dp", "context"), None),
            P("dp"),
            P("dp", "tensor"),
            P("dp", None),
            P("dp", None),
            P("dp"),
            P("dp"),
            P("tensor", "dp"),
            P("dp"),
            P("dp"),
            P("dp", "tensor"),
            P("dp", "tensor"),
            P("tensor", "dp"),
            P("dp"),
        ),
        check_vma=False,
    )
```

time: 623 us -> 349 us (0.56)
  waiting for transfers between devices: 335 us -> 126 us
  blocking collectives: 112 us -> 4.35 us
  starting transfers between devices: 30.3 us -> 70.4 us
  local copies, waits for them, and re-layouts: 32.8 us -> 50 us
  between operations: 16.5 us -> 3.18 us
  other arithmetic: 39.9 us -> 47.4 us
    psum x5 -> x0, waiting for transfers between devices: 284 us -> none  [the longest x1 168 us: local(): lax.psum((grad_ginput, grad_wquery, grad_wkey, grad_wvalue, grad_gquery,...]
    ppermute x12 -> x64, waiting for transfers between devices: 51.1 us -> 126 us  [the longest x12 39.5 us: over_context(): return lax.ppermute(array, 'context', pairs)]
    all_gather x9 -> x1, blocking collectives: 59.2 us -> 4.35 us  [local(): gain_parts = lax.all_gather(gains, 'dp', axis=0, tiled=True)]
    psum x2 -> x0, blocking collectives: 45.9 us -> none  [the longest x1 40 us: local(): lax.psum((grad_ginput, grad_wquery, grad_wkey, grad_wvalue, grad_gquery,...]
    ppermute x12 -> x64, starting transfers between devices: 29.9 us -> 70.4 us  [the longest x12 31.9 us: over_context(): return lax.ppermute(array, 'context', pairs)]
    dynamic_slice x13 -> x0, local copies, waits for them, and re-layouts: 12.6 us -> none  [local(): lax.dynamic_slice_in_dim(total_grad, shard_place * (total_grad.shape[dim_...]
    slice x0 -> x14, local copies, waits for them, and re-layouts: none -> 12.5 us  [the longest x3 4.81 us: shared(): theirs = jnp.concatenate([total[:, a:b] for a, b in other], axis=1)]
    dot_general x31 -> x14, matrix products: 24.2 us -> 11.8 us  [product(): return jnp.dot(left_side, right_side, preferred_element_type=F32)]
  transfers between devices with their start and end apart: 17 -> 64, of which waited for: 14 -> 28; matrix products, arithmetic and copies ran while one was open for 7% -> 27% of each run, Pallas kernels for 0% -> 0%
where the time goes in v1:
time: 349 us; the launch traced here: 344 us
  waiting for transfers between devices  126 us (36%)
  starting transfers between devices  70.4 us (20%)
  local copies, waits for them, and re-layouts  50 us (14%)
  other arithmetic  47.4 us (14%)
  matrix products  42.7 us (12%)
  blocking collectives  4.35 us (1%)
    ppermute x12, waiting for transfers between devices, over_context(): return lax.ppermute(array, 'context', pairs)  39.5 us
    ppermute x12, starting transfers between devices, over_context(): return lax.ppermute(array, 'context', pairs)  31.9 us
    ppermute x6, waiting for transfers between devices, over_pairs(): return lax.ppermute(array, 'tensor', [(i, i ^ 2) for i in range(devices)])  23.9 us
    unnamed x263, local copies, waits for them, and re-layouts  18.9 us
    dot_general x13, matrix products, product_lt(): lax.dot_general(left_side, right_side, (((0,), (0,)), ((), ())), preferre...  18.3 us
    ppermute x3, waiting for transfers between devices, context_sum(): part = low(keep + lax.ppermute(low(send), 'context', by_far).astype(F32))  16.2 us
    ppermute x3, waiting for transfers between devices, context_sum(): part = keep + lax.ppermute(low(send), 'context', by_near).astype(F32)  15.4 us
    ppermute x3, waiting for transfers between devices, dp_gathered(): other = lax.ppermute(array, 'dp', [(0, 1), (1, 0)])  14.2 us
  transfers between devices with their start and end apart: 64, of which 28 were waited for; matrix products, arithmetic and copies ran while one was open for 27% of the time, Pallas kernels for 0%

profile of v1, /device:TPU:0, one launch (start us, length us, event | category | flops | bytes accessed | tf_op | source)
XLA Modules:
  0.0 343.9 jit_solution(7800999672804704999)
XLA Ops:
  2.7 3.0 collective-permute-start
  7.0 4.2 %concatenate.215 = bf16[1536]{0:T(1024)(128)(2,1)S(1)} concatenate(bf16[320]{0:T(512)(128)(2,1)} %param.18, bf16[320]{0:T(512)(128)(2,1)} %param.25, bf16[320]{0:T(512)(128)(2,1)} %param.26, bf16[320]{0:T(512)(128)(2,1)} %param.30, bf16[128]{0:T(256)(128)(2,1)} %param.22, bf16[128]{0:T(256)(128)(2,1)} %param.23), dimensions={0} | concatenate | bytes 6144 | tf_op jit(solution)/shard_map/concatenate | solution.py:165
  11.2 4.4 %all-gather.1 = bf16[2,1,1536]{2,1,0:T(2,128)(2,1)S(1)} all-gather(bf16[1,1,1536]{2,1,0:T(2,128)(2,1)S(1)} %reshape.354), channel_id=2, replica_groups=mesh['dp'=2,'context'=4,'tensor'=4] {'dp'}, dimensions={0}, use_global_device_ids=true | all-gather | bytes 9216 | tf_op jit(solution)/shard_map/all_gather | solution.py:168
  20.6 4.0 %collective-permute-start.7 = (bf16[384,256]{1,0:T(8,128)(2,1)S(1)}, bf16[384,256]{1,0:T(8,128)(2,1)S(1)}, u32[]{:S(2)}, u32[]{:S(2)}) collective-permute-start(bf16[384,256]{1,0:T(8,128)(2,1)S(1)} %slice.502), channel_id=1, source_target_pairs={{0,4},{4,8},{8,12},{1,5},{5,9},{9,13},{2,6},{6,10},{10,14},{3,7},{... | collective-permute-start | bytes 589832 | tf_op jit(solution)/shard_map/ppermute | solution.py:50
  24.9 3.5 %collective-permute-start.5 = (bf16[384,256]{1,0:T(8,128)(2,1)S(1)}, bf16[384,256]{1,0:T(8,128)(2,1)S(1)}, u32[]{:S(2)}, u32[]{:S(2)}) collective-permute-start(bf16[384,256]{1,0:T(8,128)(2,1)S(1)} %pad_maximum_fusion.26), channel_id=1, source_target_pairs={{0,4},{4,8},{8,12},{1,5},{5,9},{9,13},{2,6},{6,10},{10,14},{3,7},{... | collective-permute-start | bytes 589832 | tf_op jit(solution)/shard_map/ppermute | solution.py:50
  29.0 4.2 %collective-permute-start.11 = (bf16[384,256]{1,0:T(8,128)(2,1)S(1)}, bf16[384,256]{1,0:T(8,128)(2,1)S(1)}, u32[]{:S(2)}, u32[]{:S(2)}) collective-permute-start(bf16[384,256]{1,0:T(8,128)(2,1)S(1)} %collective-permute-done.7), channel_id=1, source_target_pairs={{0,4},{4,8},{8,12},{1,5},{5,9},{9,13},{2,6},{6,10},{10,14},{3,7},{... | collective-permute-start | bytes 589832 | tf_op jit(solution)/shard_map/ppermute | solution.py:50
  33.3 3.5 %collective-permute-start.9 = (bf16[384,256]{1,0:T(8,128)(2,1)S(1)}, bf16[384,256]{1,0:T(8,128)(2,1)S(1)}, u32[]{:S(2)}, u32[]{:S(2)}) collective-permute-start(bf16[384,256]{1,0:T(8,128)(2,1)S(1)} %collective-permute-done.5), channel_id=1, source_target_pairs={{0,4},{4,8},{8,12},{1,5},{5,9},{9,13},{2,6},{6,10},{10,14},{3,7},{... | collective-permute-start | bytes 589832 | tf_op jit(solution)/shard_map/ppermute | solution.py:50
  38.5 3.1 collective-permute-done.9
  41.6 4.4 %collective-permute-start.15 = (bf16[384,256]{1,0:T(8,128)(2,1)S(1)}, bf16[384,256]{1,0:T(8,128)(2,1)S(1)}, u32[]{:S(2)}, u32[]{:S(2)}) collective-permute-start(bf16[384,256]{1,0:T(8,128)(2,1)S(1)} %collective-permute-done.11), channel_id=1, source_target_pairs={{0,4},{4,8},{8,12},{1,5},{5,9},{9,13},{2,6},{6,10},{10,14},{3,7},{... | collective-permute-start | bytes 589832 | tf_op jit(solution)/shard_map/ppermute | solution.py:50
  46.0 4.5 %collective-permute-start.13 = (bf16[384,256]{1,0:T(8,128)(2,1)S(1)}, bf16[384,256]{1,0:T(8,128)(2,1)S(1)}, u32[]{:S(2)}, u32[]{:S(2)}) collective-permute-start(bf16[384,256]{1,0:T(8,128)(2,1)S(1)} %collective-permute-done.9), channel_id=1, source_target_pairs={{0,4},{4,8},{8,12},{1,5},{5,9},{9,13},{2,6},{6,10},{10,14},{3,7},{... | collective-permute-start | bytes 589832 | tf_op jit(solution)/shard_map/ppermute | solution.py:50
  50.8 4.2 %collective-permute-done.13 = bf16[384,256]{1,0:T(8,128)(2,1)S(1)} collective-permute-done((bf16[384,256]{1,0:T(8,128)(2,1)S(1)}, bf16[384,256]{1,0:T(8,128)(2,1)S(1)}, u32[]{:S(2)}, u32[]{:S(2)}) %collective-permute-start.13) | collective-permute-done | bytes 196640 | tf_op jit(solution)/shard_map/ppermute | solution.py:50
  66.7 14.1 %collective-permute-done.18 = bf16[320,1536]{1,0:T(8,128)(2,1)S(1)} collective-permute-done((bf16[320,1536]{1,0:T(8,128)(2,1)S(1)}, bf16[320,1536]{1,0:T(8,128)(2,1)S(1)}, u32[]{:S(2)}, u32[]{:S(2)}) %collective-permute-start.18) | collective-permute-done | bytes 983072 | tf_op jit(solution)/shard_map/ppermute | solution.py:72
  80.9 2.0 maximum_select_fusion
  88.6 9.5 %collective-permute-done.17 = bf16[384,640]{1,0:T(8,128)(2,1)S(1)} collective-permute-done((bf16[384,640]{1,0:T(8,128)(2,1)S(1)}, bf16[384,640]{1,0:T(8,128)(2,1)S(1)}, u32[]{:S(2)}, u32[]{:S(2)}) %collective-permute-start.17) | collective-permute-done | bytes 491552 | tf_op jit(solution)/shard_map/ppermute | solution.py:44
  109.9 10.3 %collective-permute-done.20 = bf16[384,640]{1,0:T(8,128)(2,1)} collective-permute-done((bf16[384,640]{1,0:T(8,128)(2,1)}, bf16[384,640]{1,0:T(8,128)(2,1)}, u32[]{:S(2)}, u32[]{:S(2)}) %collective-permute-start.20) | collective-permute-done | bytes 491552 | tf_op jit(solution)/shard_map/ppermute | solution.py:44
  121.6 2.2 fusion.40
  123.9 2.5 fusion.32
  128.1 2.5 fusion.156
  130.7 2.2 fusion.25
  132.9 4.0 %fusion.29 = f32[640,2048]{1,0:T(8,128)} fusion(bf16[384,1024]{1,0:T(8,128)(2,1)S(1)} %get-tuple-element.92, bf16[384,1024]{1,0:T(8,128)(2,1)S(1)} %get-tuple-element.91, f32[384,640]{1,0:T(8,128)S(1)} %get-tuple-element.86, f32[640]{0:T(1024)S(1)} %reshape.351, f32[384]{0:T(512)S(1)} %add_rsqrt_fusion.2), kind=kOutput, calls=%fused_computation.72 | convolution fusion | flops 1010515968 | bytes 7802880 | tf_op jit(solution)/shard_map/dot_general | solution.py:22
  141.6 2.2 fusion.12
  144.3 4.6 %fusion.137 = (f32[640,512]{1,0:T(8,128)S(1)}, f32[640,512]{1,0:T(8,128)S(1)}, f32[640,512]{1,0:T(8,128)}, f32[640,512]{1,0:T(8,128)}) fusion(f32[640,2048]{1,0:T(8,128)} %fusion.29), kind=kLoop, calls=%fused_computation.339 | loop fusion | bytes 10485760 | tf_op jit(solution)/shard_map/slice | solution.py:286
  184.8 2.4 maximum_select_fusion.2
  195.1 6.4 %collective-permute-done.27 = bf16[384,256]{1,0:T(8,128)(2,1)S(1)} collective-permute-done((bf16[384,256]{1,0:T(8,128)(2,1)S(1)}, bf16[384,256]{1,0:T(8,128)(2,1)S(1)}, u32[]{:S(2)}, u32[]{:S(2)}) %collective-permute-start.27) | collective-permute-done | bytes 196640 | tf_op jit(solution)/shard_map/ppermute | solution.py:50
  203.0 7.4 %collective-permute-done.34 = bf16[384,256]{1,0:T(8,128)(2,1)S(1)} collective-permute-done((bf16[384,256]{1,0:T(8,128)(2,1)S(1)}, bf16[384,256]{1,0:T(8,128)(2,1)S(1)}, u32[]{:S(2)}, u32[]{:S(2)}) %collective-permute-start.34) | collective-permute-done | bytes 196640 | tf_op jit(solution)/shard_map/ppermute | solution.py:50
  212.8 6.9 %collective-permute-done.28 = bf16[384,256]{1,0:T(8,128)(2,1)S(1)} collective-permute-done((bf16[384,256]{1,0:T(8,128)(2,1)S(1)}, bf16[384,256]{1,0:T(8,128)(2,1)S(1)}, u32[]{:S(2)}, u32[]{:S(2)}) %collective-permute-start.28) | collective-permute-done | bytes 196640 | tf_op jit(solution)/shard_map/ppermute | solution.py:50
  221.1 7.0 %collective-permute-done.35 = bf16[384,256]{1,0:T(8,128)(2,1)S(1)} collective-permute-done((bf16[384,256]{1,0:T(8,128)(2,1)S(1)}, bf16[384,256]{1,0:T(8,128)(2,1)S(1)}, u32[]{:S(2)}, u32[]{:S(2)}) %collective-permute-start.35) | collective-permute-done | bytes 196640 | tf_op jit(solution)/shard_map/ppermute | solution.py:50
  231.3 6.1 %collective-permute-done.60 = bf16[160,512]{0,1:T(8,128)(2,1)S(1)} collective-permute-done((bf16[160,512]{0,1:T(8,128)(2,1)S(1)}, bf16[160,512]{0,1:T(8,128)(2,1)S(1)}, u32[]{:S(2)}, u32[]{:S(2)}) %collective-permute-start.60) | collective-permute-done | bytes 163872 | tf_op jit(solution)/shard_map/ppermute | solution.py:97
  237.8 2.6 collective-permute-start.61
  240.5 4.5 %collective-permute-done.61 = bf16[80,512]{0,1:T(8,128)(2,1)S(1)} collective-permute-done((bf16[80,512]{0,1:T(8,128)(2,1)S(1)}, bf16[80,512]{0,1:T(8,128)(2,1)S(1)}, u32[]{:S(2)}, u32[]{:S(2)}) %collective-permute-start.61) | collective-permute-done | bytes 81952 | tf_op jit(solution)/shard_map/ppermute | solution.py:101
  250.4 4.4 %collective-permute-done.36 = bf16[384,256]{1,0:T(8,128)(2,1)S(1)} collective-permute-done((bf16[384,256]{1,0:T(8,128)(2,1)S(1)}, bf16[384,256]{1,0:T(8,128)(2,1)S(1)}, u32[]{:S(2)}, u32[]{:S(2)}) %collective-permute-start.36) | collective-permute-done | bytes 196640 | tf_op jit(solution)/shard_map/ppermute | solution.py:50
  256.7 1.9 reduce-precision_convert_fusion.1
  261.1 2.1 collective-permute-start.48
  266.8 4.4 %collective-permute-done.48 = bf16[160,512]{0,1:T(8,128)(2,1)S(1)} collective-permute-done((bf16[160,512]{0,1:T(8,128)(2,1)S(1)}, bf16[160,512]{0,1:T(8,128)(2,1)S(1)}, u32[]{:S(2)}, u32[]{:S(2)}) %collective-permute-start.48) | collective-permute-done | bytes 163872 | tf_op jit(solution)/shard_map/ppermute | solution.py:97
  273.6 5.5 %collective-permute-done.49 = bf16[80,512]{0,1:T(8,128)(2,1)S(1)} collective-permute-done((bf16[80,512]{0,1:T(8,128)(2,1)}, bf16[80,512]{0,1:T(8,128)(2,1)S(1)}, u32[]{:S(2)}, u32[]{:S(2)}) %collective-permute-start.49) | collective-permute-done | bytes 81952 | tf_op jit(solution)/shard_map/ppermute | solution.py:101
  280.4 2.1 fusion.38
  282.6 6.5 %concatenate.253 = f32[2,336,512]{2,1,0:T(8,128)} concatenate(f32[2,320,512]{2,1,0:T(8,128)} %bitcast.74, f32[2,1,512]{2,1,0:T(1,128)S(1)} %pad.20, f32[2,1,512]{2,1,0:T(1,128)S(1)} %copy-done.118, f32[2,1,512]{2,1,0:T(1,128)S(1)} %copy-done.117, f32[2,1,512]{2,1,0:T(1,128)S(1)} %copy-done.116, f32[2,1,512]{2,1,0:T(1,128)S(1)} %pad.24, f32[2,1,512]{2,1,0:T(1,128)S(1)} %pad.25, ...), dimensions={1} | concatenate | bytes 2752512 | tf_op jit(solution)/shard_map/concatenate | solution.py:371
  290.5 2.6 fusion.37
  293.8 2.5 collective-permute-start.51
  298.8 4.6 %collective-permute-done.51 = bf16[160,512]{0,1:T(8,128)(2,1)S(1)} collective-permute-done((bf16[160,512]{0,1:T(8,128)(2,1)S(1)}, bf16[160,512]{0,1:T(8,128)(2,1)S(1)}, u32[]{:S(2)}, u32[]{:S(2)}) %collective-permute-start.51) | collective-permute-done | bytes 163872 | tf_op jit(solution)/shard_map/ppermute | solution.py:103
  305.0 4.9 %collective-permute-done.54 = bf16[160,1024]{1,0:T(8,128)(2,1)S(1)} collective-permute-done((bf16[160,1024]{1,0:T(8,128)(2,1)S(1)}, bf16[160,1024]{1,0:T(8,128)(2,1)S(1)}, u32[]{:S(2)}, u32[]{:S(2)}) %collective-permute-start.54) | collective-permute-done | bytes 327712 | tf_op jit(solution)/shard_map/ppermute | solution.py:97
  312.7 2.1 collective-permute-done.42
  314.9 3.0 collective-permute-start.43
  317.9 6.1 %collective-permute-done.55 = bf16[80,1024]{1,0:T(8,128)(2,1)S(1)} collective-permute-done((bf16[80,1024]{1,0:T(8,128)(2,1)S(1)}, bf16[80,1024]{1,0:T(8,128)(2,1)S(1)}, u32[]{:S(2)}, u32[]{:S(2)}) %collective-permute-start.55) | collective-permute-done | bytes 163872 | tf_op jit(solution)/shard_map/ppermute | solution.py:101
  327.8 2.0 collective-permute-done.44
  329.9 2.8 collective-permute-done.56
  332.9 3.7 %maximum_select_fusion.1 = f32[768,640]{1,0:T(8,128)} fusion(f32[384,640]{1,0:T(8,128)} %collective-permute-done.38, f32[384,640]{1,0:T(8,128)} %fusion.37, pred[]{:T(512)S(6)} %eq.15), kind=kLoop, calls=%fused_computation.15 | loop fusion | flops 1474560 | bytes 3932161 | tf_op jit(solution)/shard_map/jit(_where)/select_n | solution.py:58
  338.7 3.7 %collective-permute-done.57 = bf16[160,1024]{1,0:T(8,128)(2,1)S(1)} collective-permute-done((bf16[160,1024]{1,0:T(8,128)(2,1)S(1)}, bf16[160,1024]{1,0:T(8,128)(2,1)S(1)}, u32[]{:S(2)}, u32[]{:S(2)}) %collective-permute-start.57) | collective-permute-done | bytes 327712 | tf_op jit(solution)/shard_map/ppermute | solution.py:103
  (540 shorter events, 133.6 us)
Async XLA Ops:
  2.7 15.9 %collective-permute-start = (bf16[320,512]{1,0:T(8,128)(2,1)S(1)}, bf16[320,512]{1,0:T(8,128)(2,1)S(1)}, u32[]{:S(2)}, u32[]{:S(2)}) collective-permute-start(bf16[320,512]{1,0:T(8,128)(2,1)S(1)} %constant_dynamic-update-slice_fusion), channel_id=1, source_target_pairs={{0,16},{16,0},{1,17},{17,1},{2,18},{18,2},{3,19},{19,3},{4,20},{20... | collective-permute-start | bytes 983048 | tf_op jit(solution)/shard_map/ppermute | solution.py:72
  20.4 12.8 %collective-permute-start.1 = (bf16[320,512]{1,0:T(8,128)(2,1)S(1)}, bf16[320,512]{1,0:T(8,128)(2,1)S(1)}, u32[]{:S(2)}, u32[]{:S(2)}) collective-permute-start(bf16[320,512]{1,0:T(8,128)(2,1)S(1)} %pad_maximum_fusion.21), channel_id=1, source_target_pairs={{0,16},{16,0},{1,17},{17,1},{2,18},{18,2},{3,19},{19,3},{4,20},{20... | collective-permute-start | bytes 983048 | tf_op jit(solution)/shard_map/ppermute | solution.py:72
  20.6 8.4 %collective-permute-start.7 = (bf16[384,256]{1,0:T(8,128)(2,1)S(1)}, bf16[384,256]{1,0:T(8,128)(2,1)S(1)}, u32[]{:S(2)}, u32[]{:S(2)}) collective-permute-start(bf16[384,256]{1,0:T(8,128)(2,1)S(1)} %slice.502), channel_id=1, source_target_pairs={{0,4},{4,8},{8,12},{1,5},{5,9},{9,13},{2,6},{6,10},{10,14},{3,7},{... | collective-permute-start | bytes 589832 | tf_op jit(solution)/shard_map/ppermute | solution.py:50
  24.9 8.3 %collective-permute-start.5 = (bf16[384,256]{1,0:T(8,128)(2,1)S(1)}, bf16[384,256]{1,0:T(8,128)(2,1)S(1)}, u32[]{:S(2)}, u32[]{:S(2)}) collective-permute-start(bf16[384,256]{1,0:T(8,128)(2,1)S(1)} %pad_maximum_fusion.26), channel_id=1, source_target_pairs={{0,4},{4,8},{8,12},{1,5},{5,9},{9,13},{2,6},{6,10},{10,14},{3,7},{... | collective-permute-start | bytes 589832 | tf_op jit(solution)/shard_map/ppermute | solution.py:50
  28.4 35.1 %collective-permute-start.4 = (bf16[384,256]{1,0:T(8,128)(2,1)S(1)}, bf16[384,256]{1,0:T(8,128)(2,1)S(1)}, u32[]{:S(2)}, u32[]{:S(2)}) collective-permute-start(bf16[384,256]{1,0:T(8,128)(2,1)S(1)} %slice.502), channel_id=1, source_target_pairs={{0,1},{1,0},{2,3},{3,2},{4,5},{5,4},{6,7},{7,6},{8,9},{9,8},{10,11... | collective-permute-start | bytes 589832 | tf_op jit(solution)/shard_map/ppermute | solution.py:39
  28.5 33.2 %collective-permute-start.3 = (bf16[384,256]{1,0:T(8,128)(2,1)S(1)}, bf16[384,256]{1,0:T(8,128)(2,1)S(1)}, u32[]{:S(2)}, u32[]{:S(2)}) collective-permute-start(bf16[384,256]{1,0:T(8,128)(2,1)S(1)} %pad_maximum_fusion.26), channel_id=1, source_target_pairs={{0,1},{1,0},{2,3},{3,2},{4,5},{5,4},{6,7},{7,6},{8,9},{9,8},{10,11... | collective-permute-start | bytes 589832 | tf_op jit(solution)/shard_map/ppermute | solution.py:39
  29.0 9.2 %collective-permute-start.11 = (bf16[384,256]{1,0:T(8,128)(2,1)S(1)}, bf16[384,256]{1,0:T(8,128)(2,1)S(1)}, u32[]{:S(2)}, u32[]{:S(2)}) collective-permute-start(bf16[384,256]{1,0:T(8,128)(2,1)S(1)} %collective-permute-done.7), channel_id=1, source_target_pairs={{0,4},{4,8},{8,12},{1,5},{5,9},{9,13},{2,6},{6,10},{10,14},{3,7},{... | collective-permute-start | bytes 589832 | tf_op jit(solution)/shard_map/ppermute | solution.py:50
  33.2 8.4 %collective-permute-start.8 = (bf16[384,256]{1,0:T(8,128)(2,1)S(1)}, bf16[384,256]{1,0:T(8,128)(2,1)S(1)}, u32[]{:S(2)}, u32[]{:S(2)}) collective-permute-start(bf16[384,256]{1,0:T(8,128)(2,1)S(1)} %collective-permute-done.7), channel_id=1, source_target_pairs={{0,1},{1,0},{2,3},{3,2},{4,5},{5,4},{6,7},{7,6},{8,9},{9,8},{10,11... | collective-permute-start | bytes 589832 | tf_op jit(solution)/shard_map/ppermute | solution.py:39
  41.6 17.1 %collective-permute-start.2 = (bf16[640,512]{1,0:T(8,128)(2,1)S(1)}, bf16[640,512]{1,0:T(8,128)(2,1)S(1)}, u32[]{:S(2)}, u32[]{:S(2)}) collective-permute-start(bf16[640,512]{1,0:T(8,128)(2,1)S(1)} %maximum_select_fusion.4), channel_id=1, source_target_pairs={{0,1},{1,0},{2,3},{3,2},{4,5},{5,4},{6,7},{7,6},{8,9},{9,8},{10,11... | collective-permute-start | bytes 1966088 | tf_op jit(solution)/shard_map/ppermute | solution.py:39
  41.6 9.2 %collective-permute-start.15 = (bf16[384,256]{1,0:T(8,128)(2,1)S(1)}, bf16[384,256]{1,0:T(8,128)(2,1)S(1)}, u32[]{:S(2)}, u32[]{:S(2)}) collective-permute-start(bf16[384,256]{1,0:T(8,128)(2,1)S(1)} %collective-permute-done.11), channel_id=1, source_target_pairs={{0,4},{4,8},{8,12},{1,5},{5,9},{9,13},{2,6},{6,10},{10,14},{3,7},{... | collective-permute-start | bytes 589832 | tf_op jit(solution)/shard_map/ppermute | solution.py:50
  46.0 9.0 %collective-permute-start.13 = (bf16[384,256]{1,0:T(8,128)(2,1)S(1)}, bf16[384,256]{1,0:T(8,128)(2,1)S(1)}, u32[]{:S(2)}, u32[]{:S(2)}) collective-permute-start(bf16[384,256]{1,0:T(8,128)(2,1)S(1)} %collective-permute-done.9), channel_id=1, source_target_pairs={{0,4},{4,8},{8,12},{1,5},{5,9},{9,13},{2,6},{6,10},{10,14},{3,7},{... | collective-permute-start | bytes 589832 | tf_op jit(solution)/shard_map/ppermute | solution.py:50
  56.7 24.2 %collective-permute-start.18 = (bf16[320,1536]{1,0:T(8,128)(2,1)S(1)}, bf16[320,1536]{1,0:T(8,128)(2,1)S(1)}, u32[]{:S(2)}, u32[]{:S(2)}) collective-permute-start(bf16[320,1536]{1,0:T(8,128)(2,1)S(1)} %pad_maximum_fusion.5), channel_id=1, source_target_pairs={{0,16},{16,0},{1,17},{17,1},{2,18},{18,2},{3,19},{19,3},{4,20},{20... | collective-permute-start | bytes 2949128 | tf_op jit(solution)/shard_map/ppermute | solution.py:72
  82.9 17.7 %collective-permute-start.19 = (bf16[640,1536]{1,0:T(8,128)(2,1)}, bf16[640,1536]{1,0:T(8,128)(2,1)}, u32[]{:S(2)}, u32[]{:S(2)}) collective-permute-start(bf16[640,1536]{1,0:T(8,128)(2,1)} %maximum_select_fusion), channel_id=1, source_target_pairs={{0,1},{1,0},{2,3},{3,2},{4,5},{5,4},{6,7},{7,6},{8,9},{9,8},{10,11... | collective-permute-start | bytes 5898248 | tf_op jit(solution)/shard_map/ppermute | solution.py:39
  84.5 13.6 %collective-permute-start.17 = (bf16[384,640]{1,0:T(8,128)(2,1)S(1)}, bf16[384,640]{1,0:T(8,128)(2,1)S(1)}, u32[]{:S(2)}, u32[]{:S(2)}) collective-permute-start(bf16[384,640]{1,0:T(8,128)(2,1)S(1)} %fusion.24), channel_id=1, source_target_pairs={{0,2},{1,3},{2,0},{3,1},{4,6},{5,7},{6,4},{7,5},{8,10},{9,11},{10,... | collective-permute-start | bytes 1474568 | tf_op jit(solution)/shard_map/ppermute | solution.py:44
  107.0 13.2 %collective-permute-start.20 = (bf16[384,640]{1,0:T(8,128)(2,1)}, bf16[384,640]{1,0:T(8,128)(2,1)}, u32[]{:S(2)}, u32[]{:S(2)}) collective-permute-start(bf16[384,640]{1,0:T(8,128)(2,1)} %fusion.26), channel_id=1, source_target_pairs={{0,2},{1,3},{2,0},{3,1},{4,6},{5,7},{6,4},{7,5},{8,10},{9,11},{10,... | collective-permute-start | bytes 1474568 | tf_op jit(solution)/shard_map/ppermute | solution.py:44
  140.0 12.2 %collective-permute-start.22 = (bf16[384,640]{1,0:T(8,128)(2,1)}, bf16[384,640]{1,0:T(8,128)(2,1)S(1)}, u32[]{:S(2)}, u32[]{:S(2)}) collective-permute-start(bf16[384,640]{1,0:T(8,128)(2,1)} %fusion.25), channel_id=1, source_target_pairs={{0,2},{1,3},{2,0},{3,1},{4,6},{5,7},{6,4},{7,5},{8,10},{9,11},{10,... | collective-permute-start | bytes 1474568 | tf_op jit(solution)/shard_map/ppermute | solution.py:44
  141.6 42.3 %collective-permute-start.21 = (bf16[384,640]{1,0:T(8,128)(2,1)}, bf16[384,640]{1,0:T(8,128)(2,1)}, u32[]{:S(2)}, u32[]{:S(2)}) collective-permute-start(bf16[384,640]{1,0:T(8,128)(2,1)} %get-tuple-element.110), channel_id=1, source_target_pairs={{0,1},{1,0},{2,3},{3,2},{4,5},{5,4},{6,7},{7,6},{8,9},{9,8},{10,11... | collective-permute-start | bytes 1474568 | tf_op jit(solution)/shard_map/ppermute | solution.py:39
  143.8 44.0 %collective-permute-start.58 = (bf16[640,512]{0,1:T(8,128)(2,1)}, bf16[640,512]{0,1:T(8,128)(2,1)}, u32[]{:S(2)}, u32[]{:S(2)}) collective-permute-start(bf16[640,512]{0,1:T(8,128)(2,1)} %fusion.12), channel_id=1, source_target_pairs={{0,1},{1,0},{2,3},{3,2},{4,5},{5,4},{6,7},{7,6},{8,9},{9,8},{10,11... | collective-permute-start | bytes 1966088 | tf_op jit(solution)/shard_map/ppermute | solution.py:39
  150.2 113.0 %collective-permute-start.52 = (bf16[640,1024]{1,0:T(8,128)(2,1)}, bf16[640,1024]{1,0:T(8,128)(2,1)}, u32[]{:S(2)}, u32[]{:S(2)}) collective-permute-start(bf16[640,1024]{1,0:T(8,128)(2,1)} %fusion), channel_id=1, source_target_pairs={{0,1},{1,0},{2,3},{3,2},{4,5},{5,4},{6,7},{7,6},{8,9},{9,8},{10,11... | collective-permute-start | bytes 3932168 | tf_op jit(solution)/shard_map/ppermute | solution.py:39
  173.8 29.1 %collective-permute-start.32 = (bf16[384,256]{1,0:T(8,128)(2,1)S(1)}, bf16[384,256]{1,0:T(8,128)(2,1)S(1)}, u32[]{:S(2)}, u32[]{:S(2)}) collective-permute-start(bf16[384,256]{1,0:T(8,128)(2,1)S(1)} %fusion.59), channel_id=1, source_target_pairs={{0,1},{1,0},{2,3},{3,2},{4,5},{5,4},{6,7},{7,6},{8,9},{9,8},{10,11... | collective-permute-start | bytes 589832 | tf_op jit(solution)/shard_map/ppermute | solution.py:39
  174.4 18.9 %collective-permute-start.25 = (bf16[384,256]{1,0:T(8,128)(2,1)S(1)}, bf16[384,256]{1,0:T(8,128)(2,1)S(1)}, u32[]{:S(2)}, u32[]{:S(2)}) collective-permute-start(bf16[384,256]{1,0:T(8,128)(2,1)S(1)} %fusion.73), channel_id=1, source_target_pairs={{0,1},{1,0},{2,3},{3,2},{4,5},{5,4},{6,7},{7,6},{8,9},{9,8},{10,11... | collective-permute-start | bytes 589832 | tf_op jit(solution)/shard_map/ppermute | solution.py:39
  183.9 37.1 %collective-permute-start.31 = (bf16[384,256]{1,0:T(8,128)(2,1)S(1)}, bf16[384,256]{1,0:T(8,128)(2,1)S(1)}, u32[]{:S(2)}, u32[]{:S(2)}) collective-permute-start(bf16[384,256]{1,0:T(8,128)(2,1)S(1)} %fusion.63), channel_id=1, source_target_pairs={{0,1},{1,0},{2,3},{3,2},{4,5},{5,4},{6,7},{7,6},{8,9},{9,8},{10,11... | collective-permute-start | bytes 589832 | tf_op jit(solution)/shard_map/ppermute | solution.py:39
  191.9 9.6 %collective-permute-start.27 = (bf16[384,256]{1,0:T(8,128)(2,1)S(1)}, bf16[384,256]{1,0:T(8,128)(2,1)S(1)}, u32[]{:S(2)}, u32[]{:S(2)}) collective-permute-start(bf16[384,256]{1,0:T(8,128)(2,1)S(1)} %fusion.72), channel_id=1, source_target_pairs={{4,0},{8,4},{12,8},{5,1},{9,5},{13,9},{6,2},{10,6},{14,10},{7,3},{... | collective-permute-start | bytes 589832 | tf_op jit(solution)/shard_map/ppermute | solution.py:50
  193.3 17.1 %collective-permute-start.59 = (bf16[320,512]{0,1:T(8,128)(2,1)S(1)}, bf16[320,512]{0,1:T(8,128)(2,1)S(1)}, u32[]{:S(2)}, u32[]{:S(2)}) collective-permute-start(bf16[320,512]{0,1:T(8,128)(2,1)S(1)} %reduce-precision_convert_fusion.3), channel_id=1, source_target_pairs={{0,16},{16,0},{1,17},{17,1},{2,18},{18,2},{3,19},{19,3},{4,20},{20... | collective-permute-start | bytes 983048 | tf_op jit(solution)/shard_map/ppermute | solution.py:83
  201.5 8.8 %collective-permute-start.34 = (bf16[384,256]{1,0:T(8,128)(2,1)S(1)}, bf16[384,256]{1,0:T(8,128)(2,1)S(1)}, u32[]{:S(2)}, u32[]{:S(2)}) collective-permute-start(bf16[384,256]{1,0:T(8,128)(2,1)S(1)} %fusion.58), channel_id=1, source_target_pairs={{4,0},{8,4},{12,8},{5,1},{9,5},{13,9},{6,2},{10,6},{14,10},{7,3},{... | collective-permute-start | bytes 589832 | tf_op jit(solution)/shard_map/ppermute | solution.py:50
  202.9 9.3 %collective-permute-start.24 = (bf16[384,256]{1,0:T(8,128)(2,1)S(1)}, bf16[384,256]{1,0:T(8,128)(2,1)S(1)}, u32[]{:S(2)}, u32[]{:S(2)}) collective-permute-start(bf16[384,256]{1,0:T(8,128)(2,1)S(1)} %fusion.77), channel_id=1, source_target_pairs={{0,1},{1,0},{2,3},{3,2},{4,5},{5,4},{6,7},{7,6},{8,9},{9,8},{10,11... | collective-permute-start | bytes 589832 | tf_op jit(solution)/shard_map/ppermute | solution.py:39
  210.4 19.5 %collective-permute-start.46 = (bf16[640,512]{0,1:T(8,128)(2,1)S(1)}, bf16[640,512]{0,1:T(8,128)(2,1)S(1)}, u32[]{:S(2)}, u32[]{:S(2)}) collective-permute-start(bf16[640,512]{0,1:T(8,128)(2,1)S(1)} %fusion.19), channel_id=1, source_target_pairs={{0,1},{1,0},{2,3},{3,2},{4,5},{5,4},{6,7},{7,6},{8,9},{9,8},{10,11... | collective-permute-start | bytes 1966088 | tf_op jit(solution)/shard_map/ppermute | solution.py:39
  210.5 9.2 %collective-permute-start.28 = (bf16[384,256]{1,0:T(8,128)(2,1)S(1)}, bf16[384,256]{1,0:T(8,128)(2,1)S(1)}, u32[]{:S(2)}, u32[]{:S(2)}) collective-permute-start(bf16[384,256]{1,0:T(8,128)(2,1)S(1)} %fusion.76), channel_id=1, source_target_pairs={{4,0},{8,4},{12,8},{5,1},{9,5},{13,9},{6,2},{10,6},{14,10},{7,3},{... | collective-permute-start | bytes 589832 | tf_op jit(solution)/shard_map/ppermute | solution.py:50
  212.2 38.2 %collective-permute-start.30 = (bf16[384,256]{1,0:T(8,128)(2,1)S(1)}, bf16[384,256]{1,0:T(8,128)(2,1)S(1)}, u32[]{:S(2)}, u32[]{:S(2)}) collective-permute-start(bf16[384,256]{1,0:T(8,128)(2,1)S(1)} %fusion.67), channel_id=1, source_target_pairs={{0,1},{1,0},{2,3},{3,2},{4,5},{5,4},{6,7},{7,6},{8,9},{9,8},{10,11... | collective-permute-start | bytes 589832 | tf_op jit(solution)/shard_map/ppermute | solution.py:39
  219.7 8.4 %collective-permute-start.35 = (bf16[384,256]{1,0:T(8,128)(2,1)S(1)}, bf16[384,256]{1,0:T(8,128)(2,1)S(1)}, u32[]{:S(2)}, u32[]{:S(2)}) collective-permute-start(bf16[384,256]{1,0:T(8,128)(2,1)S(1)} %fusion.62), channel_id=1, source_target_pairs={{4,0},{8,4},{12,8},{5,1},{9,5},{13,9},{6,2},{10,6},{14,10},{7,3},{... | collective-permute-start | bytes 589832 | tf_op jit(solution)/shard_map/ppermute | solution.py:50
  221.0 25.7 %collective-permute-start.23 = (bf16[384,256]{1,0:T(8,128)(2,1)S(1)}, bf16[384,256]{1,0:T(8,128)(2,1)S(1)}, u32[]{:S(2)}, u32[]{:S(2)}) collective-permute-start(bf16[384,256]{1,0:T(8,128)(2,1)S(1)} %fusion.81), channel_id=1, source_target_pairs={{0,1},{1,0},{2,3},{3,2},{4,5},{5,4},{6,7},{7,6},{8,9},{9,8},{10,11... | collective-permute-start | bytes 589832 | tf_op jit(solution)/shard_map/ppermute | solution.py:39
  228.1 9.3 %collective-permute-start.60 = (bf16[160,512]{0,1:T(8,128)(2,1)S(1)}, bf16[160,512]{0,1:T(8,128)(2,1)S(1)}, u32[]{:S(2)}, u32[]{:S(2)}) collective-permute-start(bf16[160,512]{0,1:T(8,128)(2,1)S(1)} %reduce-precision_convert_fusion.7), channel_id=1, source_target_pairs={{0,4},{4,0},{8,12},{12,8},{1,5},{5,1},{9,13},{13,9},{2,6},{6,2},{1... | collective-permute-start | bytes 491528 | tf_op jit(solution)/shard_map/ppermute | solution.py:97
  229.9 18.1 %collective-permute-start.29 = (bf16[384,256]{1,0:T(8,128)(2,1)S(1)}, bf16[384,256]{1,0:T(8,128)(2,1)S(1)}, u32[]{:S(2)}, u32[]{:S(2)}) collective-permute-start(bf16[384,256]{1,0:T(8,128)(2,1)S(1)} %fusion.80), channel_id=1, source_target_pairs={{4,0},{8,4},{12,8},{5,1},{9,5},{13,9},{6,2},{10,6},{14,10},{7,3},{... | collective-permute-start | bytes 589832 | tf_op jit(solution)/shard_map/ppermute | solution.py:50
  245.1 9.8 %collective-permute-start.36 = (bf16[384,256]{1,0:T(8,128)(2,1)S(1)}, bf16[384,256]{1,0:T(8,128)(2,1)S(1)}, u32[]{:S(2)}, u32[]{:S(2)}) collective-permute-start(bf16[384,256]{1,0:T(8,128)(2,1)S(1)} %fusion.66), channel_id=1, source_target_pairs={{4,0},{8,4},{12,8},{5,1},{9,5},{13,9},{6,2},{10,6},{14,10},{7,3},{... | collective-permute-start | bytes 589832 | tf_op jit(solution)/shard_map/ppermute | solution.py:50
  246.7 13.9 %collective-permute-start.47 = (bf16[320,512]{0,1:T(8,128)(2,1)S(1)}, bf16[320,512]{0,1:T(8,128)(2,1)S(1)}, u32[]{:S(2)}, u32[]{:S(2)}) collective-permute-start(bf16[320,512]{0,1:T(8,128)(2,1)S(1)} %reduce-precision_convert_fusion.4), channel_id=1, source_target_pairs={{0,16},{16,0},{1,17},{17,1},{2,18},{18,2},{3,19},{19,3},{4,20},{20... | collective-permute-start | bytes 983048 | tf_op jit(solution)/shard_map/ppermute | solution.py:83
  248.0 12.3 %collective-permute-start.62 = (bf16[80,512]{0,1:T(8,128)(2,1)S(1)}, bf16[80,512]{0,1:T(8,128)(2,1)S(1)}, u32[]{:S(2)}, u32[]{:S(2)}) collective-permute-start(bf16[80,512]{0,1:T(8,128)(2,1)S(1)} %reduce-precision_convert_fusion.12), channel_id=1, source_target_pairs={{0,8},{4,12},{8,0},{12,4},{1,9},{5,13},{9,1},{13,5},{2,10},{6,14},... | collective-permute-start | bytes 245768 | tf_op jit(solution)/shard_map/ppermute | solution.py:102
  258.6 21.8 %collective-permute-start.37 = (bf16[384,640]{1,0:T(8,128)(2,1)}, bf16[384,640]{1,0:T(8,128)(2,1)}, u32[]{:S(2)}, u32[]{:S(2)}) collective-permute-start(bf16[384,640]{1,0:T(8,128)(2,1)} %get-tuple-element.156), channel_id=1, source_target_pairs={{0,2},{1,3},{2,0},{3,1},{4,6},{5,7},{6,4},{7,5},{8,10},{9,11},{10,... | collective-permute-start | bytes 1474568 | tf_op jit(solution)/shard_map/ppermute | solution.py:44
  260.5 11.7 %collective-permute-start.63 = (bf16[160,512]{0,1:T(8,128)(2,1)S(1)}, bf16[160,512]{0,1:T(8,128)(2,1)S(1)}, u32[]{:S(2)}, u32[]{:S(2)}) collective-permute-start(bf16[160,512]{0,1:T(8,128)(2,1)S(1)} %maximum_select_fusion.11), channel_id=1, source_target_pairs={{0,4},{4,0},{8,12},{12,8},{1,5},{5,1},{9,13},{13,9},{2,6},{6,2},{1... | collective-permute-start | bytes 491528 | tf_op jit(solution)/shard_map/ppermute | solution.py:103
  261.1 10.1 %collective-permute-start.48 = (bf16[160,512]{0,1:T(8,128)(2,1)S(1)}, bf16[160,512]{0,1:T(8,128)(2,1)S(1)}, u32[]{:S(2)}, u32[]{:S(2)}) collective-permute-start(bf16[160,512]{0,1:T(8,128)(2,1)S(1)} %reduce-precision_convert_fusion.8), channel_id=1, source_target_pairs={{0,4},{4,0},{8,12},{12,8},{1,5},{5,1},{9,13},{13,9},{2,6},{6,2},{1... | collective-permute-start | bytes 491528 | tf_op jit(solution)/shard_map/ppermute | solution.py:97
  265.9 30.5 %collective-permute-start.53 = (bf16[320,1024]{1,0:T(8,128)(2,1)}, bf16[320,1024]{1,0:T(8,128)(2,1)}, u32[]{:S(2)}, u32[]{:S(2)}) collective-permute-start(bf16[320,1024]{1,0:T(8,128)(2,1)} %reduce-precision_convert_fusion), channel_id=1, source_target_pairs={{0,16},{16,0},{1,17},{17,1},{2,18},{18,2},{3,19},{19,3},{4,20},{20... | collective-permute-start | bytes 1966088 | tf_op jit(solution)/shard_map/ppermute | solution.py:83
  280.3 13.2 %collective-permute-start.50 = (bf16[80,512]{0,1:T(8,128)(2,1)S(1)}, bf16[80,512]{0,1:T(8,128)(2,1)S(1)}, u32[]{:S(2)}, u32[]{:S(2)}) collective-permute-start(bf16[80,512]{0,1:T(8,128)(2,1)S(1)} %reduce-precision_convert_fusion.14), channel_id=1, source_target_pairs={{0,8},{4,12},{8,0},{12,4},{1,9},{5,13},{9,1},{13,5},{2,10},{6,14},... | collective-permute-start | bytes 245768 | tf_op jit(solution)/shard_map/ppermute | solution.py:102
  293.2 39.7 %collective-permute-start.38 = (f32[384,640]{1,0:T(8,128)}, f32[384,640]{1,0:T(8,128)}, u32[]{:S(2)}, u32[]{:S(2)}) collective-permute-start(f32[384,640]{1,0:T(8,128)} %fusion.37), channel_id=1, source_target_pairs={{0,1},{1,0},{2,3},{3,2},{4,5},{5,4},{6,7},{7,6},{8,9},{9,8},{10,11... | collective-permute-start | bytes 2949128 | tf_op jit(solution)/shard_map/ppermute | solution.py:39
  293.8 9.6 %collective-permute-start.51 = (bf16[160,512]{0,1:T(8,128)(2,1)S(1)}, bf16[160,512]{0,1:T(8,128)(2,1)S(1)}, u32[]{:S(2)}, u32[]{:S(2)}) collective-permute-start(bf16[160,512]{0,1:T(8,128)(2,1)S(1)} %maximum_select_fusion.10), channel_id=1, source_target_pairs={{0,4},{4,0},{8,12},{12,8},{1,5},{5,1},{9,13},{13,9},{2,6},{6,2},{1... | collective-permute-start | bytes 491528 | tf_op jit(solution)/shard_map/ppermute | solution.py:103
  298.6 11.4 %collective-permute-start.54 = (bf16[160,1024]{1,0:T(8,128)(2,1)S(1)}, bf16[160,1024]{1,0:T(8,128)(2,1)S(1)}, u32[]{:S(2)}, u32[]{:S(2)}) collective-permute-start(bf16[160,1024]{1,0:T(8,128)(2,1)S(1)} %reduce-precision_convert_fusion.6), channel_id=1, source_target_pairs={{0,4},{4,0},{8,12},{12,8},{1,5},{5,1},{9,13},{13,9},{2,6},{6,2},{1... | collective-permute-start | bytes 983048 | tf_op jit(solution)/shard_map/ppermute | solution.py:97
  311.9 12.1 %collective-permute-start.55 = (bf16[80,1024]{1,0:T(8,128)(2,1)S(1)}, bf16[80,1024]{1,0:T(8,128)(2,1)S(1)}, u32[]{:S(2)}, u32[]{:S(2)}) collective-permute-start(bf16[80,1024]{1,0:T(8,128)(2,1)S(1)} %reduce-precision_convert_fusion.11), channel_id=1, source_target_pairs={{0,8},{4,12},{8,0},{12,4},{1,9},{5,13},{9,1},{13,5},{2,10},{6,14},... | collective-permute-start | bytes 491528 | tf_op jit(solution)/shard_map/ppermute | solution.py:101
  314.9 10.3 %collective-permute-start.43 = (bf16[336,128]{1,0:T(8,128)(2,1)S(1)}, bf16[336,128]{1,0:T(8,128)(2,1)S(1)}, u32[]{:S(2)}, u32[]{:S(2)}) collective-permute-start(bf16[336,128]{1,0:T(8,128)(2,1)S(1)} %reduce-precision_convert_fusion.17), channel_id=1, source_target_pairs={{0,8},{4,12},{8,0},{12,4},{1,9},{5,13},{9,1},{13,5},{2,10},{6,14},... | collective-permute-start | bytes 258056 | tf_op jit(solution)/shard_map/ppermute | solution.py:111
  324.1 8.6 %collective-permute-start.56 = (bf16[80,1024]{1,0:T(8,128)(2,1)S(1)}, bf16[80,1024]{1,0:T(8,128)(2,1)S(1)}, u32[]{:S(2)}, u32[]{:S(2)}) collective-permute-start(bf16[80,1024]{1,0:T(8,128)(2,1)S(1)} %reduce-precision_convert_fusion.10), channel_id=1, source_target_pairs={{0,8},{4,12},{8,0},{12,4},{1,9},{5,13},{9,1},{13,5},{2,10},{6,14},... | collective-permute-start | bytes 491528 | tf_op jit(solution)/shard_map/ppermute | solution.py:102
  332.8 9.6 %collective-permute-start.57 = (bf16[160,1024]{1,0:T(8,128)(2,1)S(1)}, bf16[160,1024]{1,0:T(8,128)(2,1)S(1)}, u32[]{:S(2)}, u32[]{:S(2)}) collective-permute-start(bf16[160,1024]{1,0:T(8,128)(2,1)S(1)} %maximum_select_fusion.9), channel_id=1, source_target_pairs={{0,4},{4,0},{8,12},{12,8},{1,5},{5,1},{9,13},{13,9},{2,6},{6,2},{1... | collective-permute-start | bytes 983048 | tf_op jit(solution)/shard_map/ppermute | solution.py:103
  (141 other events, 944.4 us)
